TPU v7x, 512 devices: a whole 4x4x16 slice. The times are simulated.
512 devices in a mesh: tm: 16 (over z_lo, core), space: 32 (over y, x, z_hi).
Axes of the slice: x: 4, y: 4, z: 16 (z_hi: 2, z_lo: 8; z = z_hi * 8 + z_lo), core: 2. Of those that a mesh axis runs over, the one named last changes fastest.
Arguments:
- vectors: bfloat16 [16, 2, 32, 3, 256, 128], P('tm', None, 'space'), may hold values from -12 to 12
- gauge_links: float32 [16, 3, 2, 32, 3, 3, 128], P('tm', None, None, 'space'), may hold values from -2.5 to 2.5
- perambulator: bfloat16 [16, 256, 2, 256, 256], P('tm', 'space'), may hold values from -0.375 to 0.375
- directions: int32 [16], P('tm'), may hold values from 0 to 2
- momentum: int32 [3], replicated, may hold values from -2 to 2
- source_list: int32 [16], replicated, may hold values from 0 to 15, each once
Outputs:
- elementals: bfloat16 [16, 256, 2, 256], P('tm', 'space')
- correlator: float32 [2, 16, 16], P(None, 'tm')
Inputs may be any that keep to these rules, and one draw needn't show every extreme that they name: `directions`: 0, 1, 2 stand for x, y, z. `source_list`: each timeslice is the source of exactly one slot.
All inputs are finite; a program needn't handle non-finite values.
Results may differ from a plain program's by a relative error of at most 0.019.
Values may be sent and summed in bfloat16 or wider, within the bound.
No kernel may reach another device: no remote copies, remote signals or barrier semaphores. Data moves between devices by JAX's collectives and lax.ppermute only.
A program may use at most 64 MiB of HBM per device.

v0:
```python
import math

import jax
import jax.numpy as jnp
from jax import lax
from jax.experimental import pallas as pl
from jax.experimental.pallas import tpu as pltpu
from jax.sharding import Mesh, PartitionSpec as P


NV = 256
NS = 4
SX = 16
SY = 8
SITES = SX * SY
HALF = NV // 2
VROWS = 6 * HALF
LROWS = 64
KAPPA = 0.05

SPACE = ("y", "x", "zh")
XY = ("y", "x")
CHUNK = 16


def whole():
    return pl.BlockSpec(memory_space=pltpu.VMEM)


def scalar():
    return pl.BlockSpec(memory_space=pltpu.SMEM)


def roll_lanes(value, shift):
    return pltpu.roll(value, shift % SITES, value.ndim - 1)


def ahead_x(value, last):
    return jnp.where(last, roll_lanes(value, SX - 1), roll_lanes(value, -1))


def behind_x(value, first):
    return jnp.where(first, roll_lanes(value, 1 - SX), roll_lanes(value, 1))


def smear_kernel(pick_ref, level_ref, phase_ref, *refs):
    planes, (left_ref, right_ref, link_ref, field_ref, one_ref, two_ref) = refs[:7], refs[7:]
    for index, source in enumerate(planes):
        field_ref[index] = source[pl.ds(0, VROWS), :].astype(jnp.float32)
        link_ref[index, pl.ds(0, LROWS), :] = source[pl.ds(VROWS, LROWS), :].astype(jnp.float32)

    @pl.when(level_ref[0] != 0)
    def _():
        for plane in range(6):
            for part in range(2):
                for row in range(3):
                    for column in range(3):
                        line = link_ref[plane + 1, pl.ds(36 + part * 9 + column * 3 + row, 1), :]
                        at = pl.ds(36 + part * 9 + row * 3 + column, 1)
                        link_ref[plane, at, :] = -line if part else line

    site = lax.broadcasted_iota(jnp.int32, (18, SITES), 1) % SX
    for plane in range(1, 6):
        link_ref[plane, pl.ds(64, 18), :] = behind_x(link_ref[plane, pl.ds(0, 18), :], site == 0)
        link_ref[plane, pl.ds(88, 18), :] = roll_lanes(link_ref[plane, pl.ds(18, 18), :], SX)

    def link(plane, base):
        def get(part, row, column):
            line = link_ref[plane, pl.ds(base + part * 9 + row * 3 + column, 1), :]
            return jnp.broadcast_to(line, (CHUNK, SITES))

        return get

    def packed(matrix):
        return lambda *at: matrix(*at).astype(jnp.bfloat16)

    def apply(total, matrix, field, adjoint):
        for row in range(3):
            for column in range(3):
                if adjoint:
                    real, imag = matrix(0, column, row), matrix(1, column, row)
                    total[0][row] += real * field[0][column] + imag * field[1][column]
                    total[1][row] += real * field[1][column] - imag * field[0][column]
                else:
                    real, imag = matrix(0, row, column), matrix(1, row, column)
                    total[0][row] += real * field[0][column] - imag * field[1][column]
                    total[1][row] += real * field[1][column] + imag * field[0][column]

    column_of = lax.broadcasted_iota(jnp.int32, (CHUNK, SITES), 1) % SX
    last, first = column_of == SX - 1, column_of == 0
    pick = pick_ref[0]

    def each(field, change):
        return [[change(field[part][colour]) for colour in range(3)] for part in range(2)]

    def zeros(kind):
        zero = jnp.zeros((CHUNK, SITES), kind)
        return [[zero for _ in range(3)] for _ in range(2)]

    def narrow(field):
        return each(field, lambda v: v.astype(jnp.bfloat16))

    def sweep(plane, here, above, below):
        total = zeros(jnp.bfloat16)
        middle = narrow(here)
        apply(total, packed(link(plane, 0)), each(middle, lambda v: ahead_x(v, last)), False)
        apply(total, packed(link(plane, 64)), each(middle, lambda v: behind_x(v, first)), True)
        apply(total, packed(link(plane, 18)), each(middle, lambda v: roll_lanes(v, -SX)), False)
        apply(total, packed(link(plane, 88)), each(middle, lambda v: roll_lanes(v, SX)), True)
        apply(total, packed(link(plane, 36)), narrow(above), False)
        apply(total, packed(link(plane - 1, 36)), narrow(below), True)

        def joined(part, colour):
            return (1.0 - 6.0 * KAPPA) * here[part][colour] + KAPPA * total[part][colour].astype(jnp.float32)

        return [[joined(part, colour) for colour in range(3)] for part in range(2)]

    def step(chunk, carry):
        start = pl.multiple_of(chunk * CHUNK, CHUNK)

        def start_field(plane):
            return [
                [field_ref[plane, pl.ds((part * 3 + colour) * HALF + start, CHUNK), :] for colour in range(3)]
                for part in range(2)
            ]

        def stored(ref, plane):
            return [[ref[plane, part * 3 + colour] for colour in range(3)] for part in range(2)]

        for plane in range(1, 6):
            result = sweep(plane, start_field(plane), start_field(plane + 1), start_field(plane - 1))
            for part in range(2):
                for colour in range(3):
                    one_ref[plane, part * 3 + colour] = result[part][colour]
        for plane in range(2, 5):
            result = sweep(plane, stored(one_ref, plane), stored(one_ref, plane + 1), stored(one_ref, plane - 1))
            for part in range(2):
                for colour in range(3):
                    two_ref[plane, part * 3 + colour] = result[part][colour]
        for side in range(2):
            plane = side + 2
            here, above = stored(two_ref, plane), stored(two_ref, plane + 1)
            incoming = [
                [
                    jnp.where(
                        pick == 0,
                        ahead_x(here[part][colour], last),
                        jnp.where(pick == 1, roll_lanes(here[part][colour], -SX), above[part][colour]),
                    )
                    for colour in range(3)
                ]
                for part in range(2)
            ]
            moved = zeros(jnp.float32)
            apply(moved, link(plane, pick * 18), incoming, False)

            def row_of(index):
                return phase_ref[pl.ds(side * 4 + index, 1), :]

            for colour in range(3):

                def put(kind, part, left, real, imag):
                    index = ((kind * 2 + part) * 2 + side) * 3 + colour
                    lanes = pl.ds((index % 2) * SITES, SITES)
                    left_ref[index // 2, pl.ds(start, CHUNK), lanes] = left.astype(jnp.bfloat16)
                    right_ref[index // 2, pl.ds(start, CHUNK), lanes] = real.astype(jnp.bfloat16)
                    right_ref[index // 2, pl.ds(HALF + start, CHUNK), lanes] = imag.astype(jnp.bfloat16)

                def turned(field, base):
                    cosine, sine = row_of(base), row_of(base + 1)
                    return (
                        cosine * field[0][colour] - sine * field[1][colour],
                        cosine * field[1][colour] + sine * field[0][colour],
                    )

                real, imag = turned(moved, 0)
                put(0, 0, here[0][colour], real, imag)
                put(0, 1, here[1][colour], imag, -real)
                real, imag = turned(here, 2)
                put(1, 0, moved[0][colour], real, imag)
                put(1, 1, moved[1][colour], imag, -real)
        return carry

    lax.fori_loop(0, HALF // CHUNK, step, 0)


def room(megabytes):
    return pltpu.CompilerParams(vmem_limit_bytes=megabytes * 2**20)


def smear(pick, level, phase, *planes):
    return pl.pallas_call(
        smear_kernel,
        out_shape=(
            jax.ShapeDtypeStruct((12, HALF, 2 * SITES), jnp.bfloat16),
            jax.ShapeDtypeStruct((12, 2 * HALF, 2 * SITES), jnp.bfloat16),
        ),
        in_specs=[scalar(), scalar()] + [whole()] * (1 + len(planes)),
        out_specs=(whole(), whole()),
        scratch_shapes=[
            pltpu.VMEM((7, 112, SITES), jnp.float32),
            pltpu.VMEM((7, VROWS, SITES), jnp.float32),
            pltpu.VMEM((6, 6, CHUNK, SITES), jnp.float32),
            pltpu.VMEM((5, 6, CHUNK, SITES), jnp.float32),
        ],
        compiler_params=room(14),
        name="smear",
    )(pick, level, phase, *planes)


def pair_kernel(core_ref, own_ref, other_ref, right_ref, out_ref):
    core = core_ref[0]

    def product(ref):
        total = jnp.zeros((HALF, 2 * HALF), jnp.float32)
        for index in range(12):
            total += lax.dot_general(
                ref[index], right_ref[index], (((1,), (1,)), ((), ())), preferred_element_type=jnp.float32
            )
        return total.astype(jnp.bfloat16)

    out_ref[pl.ds(pl.multiple_of(core * HALF, HALF), HALF), :] = product(own_ref)
    out_ref[pl.ds(pl.multiple_of((1 - core) * HALF, HALF), HALF), :] = product(other_ref)


def pair(core, own, other, right):
    return pl.pallas_call(
        pair_kernel,
        out_shape=jax.ShapeDtypeStruct((NV, 2 * HALF), jnp.bfloat16),
        in_specs=[scalar(), whole(), whole(), whole()],
        out_specs=whole(),
        compiler_params=room(8),
        name="pair",
    )(core, own, other, right)


def spread_kernel(level_ref, source_ref, gathered_ref, out_ref):
    slots = source_ref.shape[0]
    for core in range(2):
        own = gathered_ref[level_ref[0] * 2 + core]
        for slot in range(slots):
            out_ref[core * slots + slot, 0] = own
            out_ref[core * slots + slot, 1] = gathered_ref[source_ref[slot]]


def spread(level, source_list, gathered):
    rows = gathered.shape[1]
    return pl.pallas_call(
        spread_kernel,
        out_shape=jax.ShapeDtypeStruct((2 * source_list.shape[0], 2, rows, 2 * HALF), jnp.bfloat16),
        in_specs=[scalar(), scalar(), whole()],
        out_specs=whole(),
        compiler_params=room(4),
        name="spread",
    )(level, source_list, gathered)


def trace_kernel(arrived_ref, block_ref, out_ref, left_ref, source_ref):
    shares, rows = arrived_ref.shape[0] // 2, arrived_ref.shape[2]
    for share in range(shares):
        at = pl.ds(share * rows, rows)
        below = pl.ds(NV + share * rows, rows)
        for half in range(2):
            for part in range(2):
                lanes = pl.ds(part * NV + half * HALF, HALF)
                source_ref[at, lanes] = arrived_ref[half * shares + share, 1, :, pl.ds(part * HALF, HALF)]
            real = arrived_ref[half * shares + share, 0, :, pl.ds(0, HALF)]
            imag = arrived_ref[half * shares + share, 0, :, pl.ds(HALF, HALF)]
            here, there = pl.ds(half * HALF, HALF), pl.ds(NV + half * HALF, HALF)
            left_ref[at, here] = real
            left_ref[at, there] = -imag
            left_ref[below, here] = imag
            left_ref[below, there] = real

    def folded(value):
        return jnp.sum(value.reshape(NV // 8, 8, NV), axis=0)

    totals = [jnp.zeros((8, NV), jnp.float32)] * 2
    for index in range(block_ref.shape[0]):
        block = block_ref[index]
        first = jnp.dot(left_ref[...], block, preferred_element_type=jnp.float32).astype(jnp.bfloat16)
        second = jnp.dot(first, source_ref[...], preferred_element_type=jnp.float32)
        second_real = second[:NV, :NV] - second[NV:, NV:]
        second_imag = second[:NV, NV:] + second[NV:, :NV]
        block_real = block[:NV].astype(jnp.float32)
        block_imag = block[NV:].astype(jnp.float32)
        totals = [
            totals[0] + folded(second_real * block_real + second_imag * block_imag),
            totals[1] + folded(second_imag * block_real - second_real * block_imag),
        ]
    lane = lax.broadcasted_iota(jnp.int32, out_ref.shape, 1)
    out_ref[...] = jnp.where(lane == 0, jnp.sum(totals[0]), jnp.sum(totals[1]))


def trace(arrived, blocks, copies):
    return pl.pallas_call(
        trace_kernel,
        out_shape=jax.ShapeDtypeStruct((copies, 128), jnp.float32),
        in_specs=[whole(), whole()],
        out_specs=whole(),
        scratch_shapes=[pltpu.VMEM((2 * NV, 2 * NV), jnp.bfloat16), pltpu.VMEM((NV, 2 * NV), jnp.bfloat16)],
        compiler_params=room(12),
        name="trace",
    )(arrived, blocks)


def phases(momentum, pick, pair_index, level, extent):
    site = jnp.arange(SITES)
    column = (site % SX).astype(jnp.float32)
    row = (site // SX).astype(jnp.float32)
    moment = momentum.astype(jnp.float32)
    height = (pair_index * 2 + jnp.stack([level, 1 - level])).astype(jnp.float32)
    angle = (
        2.0
        * math.pi
        * (moment[0] * column[None] / SX + moment[1] * row[None] / SY + moment[2] * height[:, None] / extent)
    )
    step = jnp.where(pick == 0, moment[0] / SX, jnp.where(pick == 1, moment[1] / SY, moment[2] / extent))
    sign = jnp.where((level != 0) & (pick == 2), -1.0, 1.0)
    shifted = angle + sign * (2.0 * math.pi) * step
    turns = [jnp.cos(angle), -jnp.sin(angle), -jnp.cos(shifted), jnp.sin(shifted)]
    return (sign * jnp.stack(turns, axis=1)).reshape(8, SITES)


def per_device(vectors, gauge_links, perambulator, directions, momentum, source_list):
    core = lax.axis_index("core")
    level = lax.axis_index("zh")
    pair_index = lax.axis_index(XY)
    pairs = lax.axis_size(XY)
    rows = NV // pairs

    links = gauge_links[0, :, :, 0].reshape(54, SITES).astype(jnp.bfloat16)
    pick_row = jnp.broadcast_to(directions[0].astype(jnp.bfloat16), (LROWS - 54, SITES))
    tail = jnp.concatenate([links, pick_row], axis=0)
    planes_here = vectors[0, :, 0].reshape(6, NV, SITES)
    sites = ("core", "zh")
    same = core == level

    def half_of(index):
        half = lax.dynamic_slice_in_dim(planes_here, index * HALF, HALF, 1).reshape(VROWS, SITES)
        return jnp.concatenate([half, tail], axis=0)

    first_half, second_half = lax.optimization_barrier((half_of(core), half_of(1 - core)))
    cross_sibling = lax.ppermute(second_half, sites, [(1, 2), (2, 1)])
    cross_same = lax.ppermute(first_half, sites, [(1, 0), (2, 3)])

    def moved(plane, distance):
        route = [
            (i * 2 + z, (i + (distance if z == 0 else -distance)) % pairs * 2 + z) for i in range(pairs) for z in (0, 1)
        ]
        return lax.ppermute(plane, SPACE, route)

    taken = lax.ppermute(second_half, sites, [(0, 2), (3, 1)])
    own = jnp.where(same, first_half, taken)
    row_own = (moved(own, 1), own, moved(own, -1), moved(own, -2))
    other = jnp.where(same, cross_same, cross_sibling)
    row_other = (moved(other, 1), other, moved(other, -1))
    planes = [row_own[0], row_other[0], row_own[1], row_other[1], row_own[2], row_other[2], row_own[3]]
    pick = row_own[1][VROWS + 54, 0].astype(jnp.int32)
    phase = phases(momentum, pick, pair_index, level, 2 * pairs)
    left, right = smear(pick[None], level[None], phase, *planes)
    sibling = lax.ppermute(left, "core", [(0, 1), (1, 0)])
    partial_value = pair(core[None], left, sibling, right)

    parts = lax.all_to_all(partial_value, XY, 0, 0, tiled=True).reshape(pairs, rows, 2 * HALF)
    scale = 1.0 / math.sqrt(3 * SITES * 2 * pairs)
    share = (jnp.sum(parts.astype(jnp.float32), axis=0) * scale).astype(jnp.bfloat16)

    slices = lax.axis_size(("zl", "zh"))
    copies = jnp.broadcast_to(share[None], (slices, rows, 2 * HALF))
    gathered = lax.all_to_all(copies, ("zl", "zh"), 0, 0, tiled=True)
    sent = spread(lax.axis_index("zl")[None], source_list, gathered)
    arrived = lax.all_to_all(sent, ("core", "y", "x"), 0, 0, tiled=True)

    space_count = lax.axis_size(SPACE)
    blocks = perambulator[0].reshape(-1, 2 * NV, NV)
    value = trace(arrived, blocks, space_count)
    values = lax.all_to_all(value, SPACE, 0, 0, tiled=True)[:, :2].reshape(pairs, 2, 2)
    per_slot = jnp.sum(values, axis=1) / (NS * NV)
    one_hot = (source_list[:, None] == jnp.arange(source_list.shape[0])[None]).astype(jnp.float32)
    correlator = jnp.sum(per_slot[:, :, None] * one_hot[:, None, :], axis=0)

    own_rows = NV // space_count
    mine = lax.dynamic_index_in_dim(arrived.reshape(2, pairs, 2, rows, 2, HALF)[:, :, 0], pair_index, 1, keepdims=False)
    mine = lax.dynamic_slice_in_dim(mine, level * own_rows, own_rows, 1)
    elemental = jnp.transpose(mine, (1, 2, 0, 3)).reshape(1, own_rows, 2, NV)
    return elemental, correlator[:, None, :]


def solution(mesh):
    grid = Mesh(mesh.devices.reshape(8, 2, 4, 4, 2), ("zl", "core", "y", "x", "zh"))
    times = ("zl", "core")
    in_specs = (
        P(times, None, SPACE, None, None, None),
        P(times, None, None, SPACE, None, None, None),
        P(times, SPACE, None, None, None),
        P(times),
        P(),
        P(),
    )
    out_specs = (P(times, SPACE, None, None), P(None, times, None))

    return jax.shard_map(per_device, mesh=grid, in_specs=in_specs, out_specs=out_specs, check_vma=False)
```

profile of v0, /device:TPU:32, one launch (start us, length us, event | category | flops | bytes accessed | tf_op | source)
XLA Modules:
  0.0 160.9 jit_solution(6804069650622504420)
XLA Ops:
  2.2 1.0 constant_dynamic-slice_fusion.1
  4.2 16.2 %collective-permute-start = (bf16[832,128]{1,0:T(8,128)(2,1)S(1)}, bf16[832,128]{1,0:T(8,128)(2,1)S(1)}, u32[]{:S(2)}, u32[]{:S(2)}) collective-permute-start(bf16[832,128]{1,0:T(8,128)(2,1)S(1)} %get-tuple-element.7), channel_id=1, source_target_pairs={{0,32},{33,1},{2,34},{35,3},{4,36},{37,5},{6,38},{39,7},{8,40},{41... | collective-permute-start | bytes 638984 | tf_op jit(solution)/shard_map/ppermute | solution.py:353
  20.3 1.3 collective-permute-start.2
  24.8 1.2 fusion.9
  26.7 16.9 %collective-permute-done.2 = bf16[832,128]{1,0:T(8,128)(2,1)S(1)} collective-permute-done((bf16[832,128]{1,0:T(8,128)(2,1)S(1)}, bf16[832,128]{1,0:T(8,128)(2,1)S(1)}, u32[]{:S(2)}, u32[]{:S(2)}) %collective-permute-start.2) | collective-permute-done | bytes 213024 | tf_op jit(solution)/shard_map/ppermute | solution.py:345
  43.7 3.4 %collective-permute-start.4 = (bf16[832,128]{1,0:T(8,128)(2,1)S(1)}, bf16[832,128]{1,0:T(8,128)(2,1)S(1)}, u32[]{:S(2)}, u32[]{:S(2)}) collective-permute-start(bf16[832,128]{1,0:T(8,128)(2,1)S(1)} %broadcast_select_fusion.refs_3_), channel_id=1, source_target_pairs={{0,2},{1,31},{2,4},{3,1},{4,6},{5,3},{6,8},{7,5},{8,10},{9,7},{10,... | collective-permute-start | bytes 638984 | tf_op jit(solution)/shard_map/ppermute | solution.py:351
  47.1 5.8 %collective-permute-start.6 = (bf16[832,128]{1,0:T(8,128)(2,1)S(1)}, bf16[832,128]{1,0:T(8,128)(2,1)S(1)}, u32[]{:S(2)}, u32[]{:S(2)}) collective-permute-start(bf16[832,128]{1,0:T(8,128)(2,1)S(1)} %broadcast_select_fusion.refs_3_), channel_id=1, source_target_pairs={{0,30},{1,3},{2,0},{3,5},{4,2},{5,7},{6,4},{7,9},{8,6},{9,11},{10,... | collective-permute-start | bytes 638984 | tf_op jit(solution)/shard_map/ppermute | solution.py:351
  52.9 1.9 %collective-permute-start.1 = (bf16[832,128]{1,0:T(8,128)(2,1)S(1)}, bf16[832,128]{1,0:T(8,128)(2,1)S(1)}, u32[]{:S(2)}, u32[]{:S(2)}) collective-permute-start(bf16[832,128]{1,0:T(8,128)(2,1)S(1)} %broadcast_select_fusion.1.refs_2_), channel_id=1, source_target_pairs={{0,2},{1,31},{2,4},{3,1},{4,6},{5,3},{6,8},{7,5},{8,10},{9,7},{10,... | collective-permute-start | bytes 638984 | tf_op jit(solution)/shard_map/ppermute | solution.py:351
  54.8 7.2 %collective-permute-start.5 = (bf16[832,128]{1,0:T(8,128)(2,1)S(1)}, bf16[832,128]{1,0:T(8,128)(2,1)S(1)}, u32[]{:S(2)}, u32[]{:S(2)}) collective-permute-start(bf16[832,128]{1,0:T(8,128)(2,1)S(1)} %broadcast_select_fusion.1.refs_2_), channel_id=1, source_target_pairs={{0,30},{1,3},{2,0},{3,5},{4,2},{5,7},{6,4},{7,9},{8,6},{9,11},{10,... | collective-permute-start | bytes 638984 | tf_op jit(solution)/shard_map/ppermute | solution.py:351
  62.1 1.9 %collective-permute-start.7 = (bf16[832,128]{1,0:T(8,128)(2,1)S(1)}, bf16[832,128]{1,0:T(8,128)(2,1)S(1)}, u32[]{:S(2)}, u32[]{:S(2)}) collective-permute-start(bf16[832,128]{1,0:T(8,128)(2,1)S(1)} %broadcast_select_fusion.1.refs_2_), channel_id=1, source_target_pairs={{0,28},{1,5},{2,30},{3,7},{4,0},{5,9},{6,2},{7,11},{8,4},{9,13},{1... | collective-permute-start | bytes 638984 | tf_op jit(solution)/shard_map/ppermute | solution.py:351
  65.7 5.7 %collective-permute-done.7.refs_6_ = bf16[832,128]{1,0:T(8,128)(2,1)S(1)} collective-permute-done((bf16[832,128]{1,0:T(8,128)(2,1)S(1)}, bf16[832,128]{1,0:T(8,128)(2,1)S(1)}, u32[]{:S(2)}, u32[]{:S(2)}) %collective-permute-start.7) | collective-permute-done | bytes 213024 | tf_op jit(solution)/shard_map/ppermute | solution.py:351
  71.3 6.8 %smear.1 = (bf16[12,128,256]{2,1,0:T(8,128)(2,1)S(1)}, bf16[12,256,256]{2,1,0:T(8,128)(2,1)S(1)}) custom-call(s32[1]{0:T(128)} %bitcast.6.pick_ref, s32[1]{0:T(128)} %bitcast.7.level_ref, f32[8,128]{1,0:T(8,128)S(1)} %bitcast.36, bf16[832,128]{1,0:T(8,128)(2,1)S(1)} %collective-permute-done.1.refs_0_, bf16[832,128]{1,0:T(8,128)(2,1)S(1)} %collective-permute-done.4.refs_1_, ...), custom_call_target="tpu_custom_call" | custom-call | tf_op jit(solution)/shard_map/smear/pallas_call | solution.py:192
  78.1 1.9 %collective-permute-start.8 = (bf16[12,128,256]{2,1,0:T(8,128)(2,1)S(1)}, bf16[12,128,256]{2,1,0:T(8,128)(2,1)S(1)}, u32[]{:S(2)}, u32[]{:S(2)}) collective-permute-start(bf16[12,128,256]{2,1,0:T(8,128)(2,1)S(1)} %get-tuple-element.8.own_ref), channel_id=1, source_target_pairs={{0,32},{32,0},{1,33},{33,1},{2,34},{34,2},{3,35},{35,3},{4,36},{36... | collective-permute-start | bytes 2359304 | tf_op jit(solution)/shard_map/ppermute | solution.py:362
  80.1 2.3 %collective-permute-done.8.other_ref = bf16[12,128,256]{2,1,0:T(8,128)(2,1)S(1)} collective-permute-done((bf16[12,128,256]{2,1,0:T(8,128)(2,1)S(1)}, bf16[12,128,256]{2,1,0:T(8,128)(2,1)S(1)}, u32[]{:S(2)}, u32[]{:S(2)}) %collective-permute-start.8) | collective-permute-done | bytes 786464 | tf_op jit(solution)/shard_map/ppermute | solution.py:362
  82.3 1.1 pair.1
  83.5 11.5 %all_to_all.31 = bf16[16,16,256]{2,1,0:T(8,128)(2,1)S(1)} all-to-all(bf16[16,16,256]{2,1,0:T(8,128)(2,1)S(1)} %bitcast.35), channel_id=1, replica_groups=mesh['zl'=8,'core'=2,'y'=4,'x'=4,'zh'=2] {'y','x'}, dimensions={0} | all-to-all | bytes 262144 | tf_op jit(solution)/shard_map/all_to_all | solution.py:365
  95.6 7.5 %all-to-all-start.1 = ((bf16[16,16,256]{2,1,0:T(8,128)(2,1)}), bf16[16,16,256]{2,1,0:T(8,128)(2,1)S(1)}, u32[]{:S(2)}, u32[]{:S(2)}) async-start(bf16[16,16,256]{2,1,0:T(8,128)(2,1)} %broadcast_in_dim.36), calls=%async_computation.1 | async-start | bytes 262144 | tf_op jit(solution)/shard_map/all_to_all | solution.py:371
  103.2 14.9 %all-to-all-done.1.gathered_ref = bf16[16,16,256]{2,1,0:T(8,128)(2,1)S(1)} async-done(((bf16[16,16,256]{2,1,0:T(8,128)(2,1)}), bf16[16,16,256]{2,1,0:T(8,128)(2,1)S(1)}, u32[]{:S(2)}, u32[]{:S(2)}) %all-to-all-start.1) | async-done | bytes 131104 | tf_op jit(solution)/shard_map/all_to_all | solution.py:371
  118.1 1.4 spread.1
  119.4 3.9 %all-to-all-start.2 = ((bf16[32,2,16,256]{3,2,1,0:T(8,128)(2,1)}), bf16[32,2,16,256]{3,2,1,0:T(8,128)(2,1)S(1)}, u32[]{:S(2)}, u32[]{:S(2)}) async-start(bf16[32,2,16,256]{3,2,1,0:T(8,128)(2,1)} %spread.1), calls=%async_computation.2 | async-start | bytes 1048576 | tf_op jit(solution)/shard_map/all_to_all | solution.py:373
  123.4 11.9 %all-to-all-done.2.arrived_ref = bf16[32,2,16,256]{3,2,1,0:T(8,128)(2,1)S(1)} async-done(((bf16[32,2,16,256]{3,2,1,0:T(8,128)(2,1)}), bf16[32,2,16,256]{3,2,1,0:T(8,128)(2,1)S(1)}, u32[]{:S(2)}, u32[]{:S(2)}) %all-to-all-start.2) | async-done | bytes 524320 | tf_op jit(solution)/shard_map/all_to_all | solution.py:373
  135.6 3.7 %trace.1 = f32[32,128]{1,0:T(8,128)} custom-call(bf16[32,2,16,256]{3,2,1,0:T(8,128)(2,1)S(1)} %all-to-all-done.2.arrived_ref, bf16[8,512,256]{2,1,0:T(8,128)(2,1)S(1)} %bitcast.34), custom_call_target="tpu_custom_call" | custom-call | tf_op jit(solution)/shard_map/trace/pallas_call | solution.py:296
  139.4 3.8 %all-to-all-start.3 = ((f32[32,1,128]{2,1,0:T(1,128)}), f32[32,1,128]{2,1,0:T(1,128)S(1)}, u32[]{:S(2)}, u32[]{:S(2)}) async-start(f32[32,1,128]{2,1,0:T(1,128)} %bitcast.21), calls=%async_computation.3 | async-start | bytes 32768 | tf_op jit(solution)/shard_map/all_to_all | solution.py:378
  143.8 16.3 %all-to-all-done.3 = f32[32,1,128]{2,1,0:T(1,128)S(1)} async-done(((f32[32,1,128]{2,1,0:T(1,128)}), f32[32,1,128]{2,1,0:T(1,128)S(1)}, u32[]{:S(2)}, u32[]{:S(2)}) %all-to-all-start.3) | async-done | bytes 16416 | tf_op jit(solution)/shard_map/all_to_all | solution.py:378
  (39 shorter events, 7.3 us)
Async XLA Ops:
  3.5 40.2 %collective-permute-start.3 = (bf16[832,128]{1,0:T(8,128)(2,1)S(1)}, bf16[832,128]{1,0:T(8,128)(2,1)S(1)}, u32[]{:S(2)}, u32[]{:S(2)}) collective-permute-start(bf16[832,128]{1,0:T(8,128)(2,1)S(1)} %get-tuple-element.7), channel_id=1, source_target_pairs={{1,32},{32,1},{3,34},{34,3},{5,36},{36,5},{7,38},{38,7},{9,40},{40... | collective-permute-start | bytes 638984 | tf_op jit(solution)/shard_map/ppermute | solution.py:344
  4.2 48.7 %collective-permute-start = (bf16[832,128]{1,0:T(8,128)(2,1)S(1)}, bf16[832,128]{1,0:T(8,128)(2,1)S(1)}, u32[]{:S(2)}, u32[]{:S(2)}) collective-permute-start(bf16[832,128]{1,0:T(8,128)(2,1)S(1)} %get-tuple-element.7), channel_id=1, source_target_pairs={{0,32},{33,1},{2,34},{35,3},{4,36},{37,5},{6,38},{39,7},{8,40},{41... | collective-permute-start | bytes 638984 | tf_op jit(solution)/shard_map/ppermute | solution.py:353
  20.3 23.3 %collective-permute-start.2 = (bf16[832,128]{1,0:T(8,128)(2,1)S(1)}, bf16[832,128]{1,0:T(8,128)(2,1)S(1)}, u32[]{:S(2)}, u32[]{:S(2)}) collective-permute-start(bf16[832,128]{1,0:T(8,128)(2,1)S(1)} %get-tuple-element.6), channel_id=1, source_target_pairs={{1,0},{32,33},{3,2},{34,35},{5,4},{36,37},{7,6},{38,39},{9,8},{40,... | collective-permute-start | bytes 638984 | tf_op jit(solution)/shard_map/ppermute | solution.py:345
  43.7 21.7 %collective-permute-start.4 = (bf16[832,128]{1,0:T(8,128)(2,1)S(1)}, bf16[832,128]{1,0:T(8,128)(2,1)S(1)}, u32[]{:S(2)}, u32[]{:S(2)}) collective-permute-start(bf16[832,128]{1,0:T(8,128)(2,1)S(1)} %broadcast_select_fusion.refs_3_), channel_id=1, source_target_pairs={{0,2},{1,31},{2,4},{3,1},{4,6},{5,3},{6,8},{7,5},{8,10},{9,7},{10,... | collective-permute-start | bytes 638984 | tf_op jit(solution)/shard_map/ppermute | solution.py:351
  47.1 18.3 %collective-permute-start.6 = (bf16[832,128]{1,0:T(8,128)(2,1)S(1)}, bf16[832,128]{1,0:T(8,128)(2,1)S(1)}, u32[]{:S(2)}, u32[]{:S(2)}) collective-permute-start(bf16[832,128]{1,0:T(8,128)(2,1)S(1)} %broadcast_select_fusion.refs_3_), channel_id=1, source_target_pairs={{0,30},{1,3},{2,0},{3,5},{4,2},{5,7},{6,4},{7,9},{8,6},{9,11},{10,... | collective-permute-start | bytes 638984 | tf_op jit(solution)/shard_map/ppermute | solution.py:351
  52.9 12.8 %collective-permute-start.1 = (bf16[832,128]{1,0:T(8,128)(2,1)S(1)}, bf16[832,128]{1,0:T(8,128)(2,1)S(1)}, u32[]{:S(2)}, u32[]{:S(2)}) collective-permute-start(bf16[832,128]{1,0:T(8,128)(2,1)S(1)} %broadcast_select_fusion.1.refs_2_), channel_id=1, source_target_pairs={{0,2},{1,31},{2,4},{3,1},{4,6},{5,3},{6,8},{7,5},{8,10},{9,7},{10,... | collective-permute-start | bytes 638984 | tf_op jit(solution)/shard_map/ppermute | solution.py:351
  54.8 10.8 %collective-permute-start.5 = (bf16[832,128]{1,0:T(8,128)(2,1)S(1)}, bf16[832,128]{1,0:T(8,128)(2,1)S(1)}, u32[]{:S(2)}, u32[]{:S(2)}) collective-permute-start(bf16[832,128]{1,0:T(8,128)(2,1)S(1)} %broadcast_select_fusion.1.refs_2_), channel_id=1, source_target_pairs={{0,30},{1,3},{2,0},{3,5},{4,2},{5,7},{6,4},{7,9},{8,6},{9,11},{10,... | collective-permute-start | bytes 638984 | tf_op jit(solution)/shard_map/ppermute | solution.py:351
  62.1 9.2 %collective-permute-start.7 = (bf16[832,128]{1,0:T(8,128)(2,1)S(1)}, bf16[832,128]{1,0:T(8,128)(2,1)S(1)}, u32[]{:S(2)}, u32[]{:S(2)}) collective-permute-start(bf16[832,128]{1,0:T(8,128)(2,1)S(1)} %broadcast_select_fusion.1.refs_2_), channel_id=1, source_target_pairs={{0,28},{1,5},{2,30},{3,7},{4,0},{5,9},{6,2},{7,11},{8,4},{9,13},{1... | collective-permute-start | bytes 638984 | tf_op jit(solution)/shard_map/ppermute | solution.py:351
  78.1 39.9 %copy-start.1 = (s32[16]{0:T(128)S(1)}, s32[16]{0:T(128)}, u32[]{:S(2)}) copy-start(s32[16]{0:T(128)} %source_ref.1) | copy-start | bytes 196
  78.1 4.2 %collective-permute-start.8 = (bf16[12,128,256]{2,1,0:T(8,128)(2,1)S(1)}, bf16[12,128,256]{2,1,0:T(8,128)(2,1)S(1)}, u32[]{:S(2)}, u32[]{:S(2)}) collective-permute-start(bf16[12,128,256]{2,1,0:T(8,128)(2,1)S(1)} %get-tuple-element.8.own_ref), channel_id=1, source_target_pairs={{0,32},{32,0},{1,33},{33,1},{2,34},{34,2},{3,35},{35,3},{4,36},{36... | collective-permute-start | bytes 2359304 | tf_op jit(solution)/shard_map/ppermute | solution.py:362
  83.5 52.2 %copy-start = (bf16[1,8,2,256,256]{4,3,2,1,0:T(8,128)(2,1)S(1)}, bf16[1,8,2,256,256]{4,3,2,1,0:T(8,128)(2,1)}, u32[]{:S(2)}) copy-start(bf16[1,8,2,256,256]{4,3,2,1,0:T(8,128)(2,1)} %param.8) | copy-start | bytes 6291460
  95.6 22.4 %all-to-all-start.1 = ((bf16[16,16,256]{2,1,0:T(8,128)(2,1)}), bf16[16,16,256]{2,1,0:T(8,128)(2,1)S(1)}, u32[]{:S(2)}, u32[]{:S(2)}) async-start(bf16[16,16,256]{2,1,0:T(8,128)(2,1)} %broadcast_in_dim.36), calls=%async_computation.1 | async-start | bytes 262144 | tf_op jit(solution)/shard_map/all_to_all | solution.py:371
  119.4 15.9 %all-to-all-start.2 = ((bf16[32,2,16,256]{3,2,1,0:T(8,128)(2,1)}), bf16[32,2,16,256]{3,2,1,0:T(8,128)(2,1)S(1)}, u32[]{:S(2)}, u32[]{:S(2)}) async-start(bf16[32,2,16,256]{3,2,1,0:T(8,128)(2,1)} %spread.1), calls=%async_computation.2 | async-start | bytes 1048576 | tf_op jit(solution)/shard_map/all_to_all | solution.py:373
  139.4 20.8 %all-to-all-start.3 = ((f32[32,1,128]{2,1,0:T(1,128)}), f32[32,1,128]{2,1,0:T(1,128)S(1)}, u32[]{:S(2)}, u32[]{:S(2)}) async-start(f32[32,1,128]{2,1,0:T(1,128)} %bitcast.21), calls=%async_computation.3 | async-start | bytes 32768 | tf_op jit(solution)/shard_map/all_to_all | solution.py:378
where the time goes:
time: 162 us; the launch traced here: 161 us
  waiting for transfers between devices  68.2 us (42%)
  starting transfers between devices  55.5 us (34%)
  Pallas kernels  13 us (8%)
  blocking collectives  11.5 us (7%)
  other arithmetic  4.53 us (3%)
  local copies, waits for them, and re-layouts  4.09 us (3%)
  between operations  4.06 us (3%)
    ppermute x5, starting transfers between devices, moved(): return lax.ppermute(plane, SPACE, route)  20.2 us
    ppermute x1, waiting for transfers between devices, per_device(): cross_same = lax.ppermute(first_half, sites, [(1, 0), (2, 3)])  16.9 us
    all_to_all x1, waiting for transfers between devices, per_device(): lax.all_to_all(value, SPACE, 0, 0, tiled=True)[:, :2].reshape(pairs, 2, 2)  16.3 us
    ppermute x1, starting transfers between devices, per_device(): taken = lax.ppermute(second_half, sites, [(0, 2), (3, 1)])  16.2 us
    all_to_all x1, waiting for transfers between devices, per_device(): gathered = lax.all_to_all(copies, ('zl', 'zh'), 0, 0, tiled=True)  14.9 us
    all_to_all x1, waiting for transfers between devices, per_device(): arrived = lax.all_to_all(sent, ('core', 'y', 'x'), 0, 0, tiled=True)  11.9 us
    all_to_all x1, blocking collectives, per_device(): lax.all_to_all(partial_value, XY, 0, 0, tiled=True)  11.5 us
    all_to_all x1, starting transfers between devices, per_device(): gathered = lax.all_to_all(copies, ('zl', 'zh'), 0, 0, tiled=True)  7.53 us
  transfers between devices with their start and end apart: 12, of which 7 were waited for; matrix products, arithmetic and copies ran while one was open for 3% of the time, Pallas kernels for 0%

commit v1 on v0

--- a/solution.py
+++ b/solution.py
@@ -1,3 +1,4 @@
+import functools
 import math
 
 import jax
@@ -21,6 +22,9 @@
 SPACE = ("y", "x", "zh")
 XY = ("y", "x")
 CHUNK = 16
+PARTS = 2
+PART = HALF // PARTS
+PROWS = 6 * PART
 
 
 def whole():
@@ -43,11 +47,20 @@
     return jnp.where(first, roll_lanes(value, 1 - SX), roll_lanes(value, 1))
 
 
-def smear_kernel(pick_ref, level_ref, phase_ref, *refs):
-    planes, (left_ref, right_ref, link_ref, field_ref, one_ref, two_ref) = refs[:7], refs[7:]
-    for index, source in enumerate(planes):
-        field_ref[index] = source[pl.ds(0, VROWS), :].astype(jnp.float32)
-        link_ref[index, pl.ds(0, LROWS), :] = source[pl.ds(VROWS, LROWS), :].astype(jnp.float32)
+def smear_kernel(turn, pick_ref, level_ref, phase_ref, *refs):
+    own, other, tails = refs[0:4], refs[4:7], refs[7:10]
+    left_ref, right_ref, link_ref, field_ref, one_ref, two_ref = refs[10:]
+    for index in range(7):
+        if index % 2:
+            field_ref[index] = other[index // 2][pl.ds(0, PROWS), :].astype(jnp.float32)
+            links = tails[index // 2][pl.ds(PROWS, LROWS), :]
+        else:
+            source = own[index // 2]
+            for field in range(6):
+                rows = source[pl.ds(field * HALF + turn * PART, PART), :]
+                field_ref[index, pl.ds(field * PART, PART), :] = rows.astype(jnp.float32)
+            links = source[pl.ds(VROWS, LROWS), :]
+        link_ref[index, pl.ds(0, LROWS), :] = links.astype(jnp.float32)
 
     @pl.when(level_ref[0] != 0)
     def _():
@@ -120,7 +133,7 @@
 
         def start_field(plane):
             return [
-                [field_ref[plane, pl.ds((part * 3 + colour) * HALF + start, CHUNK), :] for colour in range(3)]
+                [field_ref[plane, pl.ds((part * 3 + colour) * PART + start, CHUNK), :] for colour in range(3)]
                 for part in range(2)
             ]
 
@@ -164,7 +177,7 @@
                     lanes = pl.ds((index % 2) * SITES, SITES)
                     left_ref[index // 2, pl.ds(start, CHUNK), lanes] = left.astype(jnp.bfloat16)
                     right_ref[index // 2, pl.ds(start, CHUNK), lanes] = real.astype(jnp.bfloat16)
-                    right_ref[index // 2, pl.ds(HALF + start, CHUNK), lanes] = imag.astype(jnp.bfloat16)
+                    right_ref[index // 2, pl.ds(PART + start, CHUNK), lanes] = imag.astype(jnp.bfloat16)
 
                 def turned(field, base):
                     cosine, sine = row_of(base), row_of(base + 1)
@@ -181,57 +194,62 @@
                 put(1, 1, moved[1][colour], imag, -real)
         return carry
 
-    lax.fori_loop(0, HALF // CHUNK, step, 0)
+    lax.fori_loop(0, PART // CHUNK, step, 0)
 
 
 def room(megabytes):
     return pltpu.CompilerParams(vmem_limit_bytes=megabytes * 2**20)
 
 
-def smear(pick, level, phase, *planes):
+def smear(turn, pick, level, phase, own, other, tails):
+    planes = (*own, *other, *tails)
     return pl.pallas_call(
-        smear_kernel,
+        functools.partial(smear_kernel, turn),
         out_shape=(
-            jax.ShapeDtypeStruct((12, HALF, 2 * SITES), jnp.bfloat16),
-            jax.ShapeDtypeStruct((12, 2 * HALF, 2 * SITES), jnp.bfloat16),
+            jax.ShapeDtypeStruct((12, PART, 2 * SITES), jnp.bfloat16),
+            jax.ShapeDtypeStruct((12, 2 * PART, 2 * SITES), jnp.bfloat16),
         ),
         in_specs=[scalar(), scalar()] + [whole()] * (1 + len(planes)),
         out_specs=(whole(), whole()),
         scratch_shapes=[
             pltpu.VMEM((7, 112, SITES), jnp.float32),
-            pltpu.VMEM((7, VROWS, SITES), jnp.float32),
+            pltpu.VMEM((7, PROWS, SITES), jnp.float32),
             pltpu.VMEM((6, 6, CHUNK, SITES), jnp.float32),
             pltpu.VMEM((5, 6, CHUNK, SITES), jnp.float32),
         ],
-        compiler_params=room(14),
+        compiler_params=room(12),
+        cost_estimate=pl.CostEstimate(flops=10**7, bytes_accessed=10**7, transcendentals=0),
         name="smear",
     )(pick, level, phase, *planes)
 
 
-def pair_kernel(core_ref, own_ref, other_ref, right_ref, out_ref):
-    core = core_ref[0]
-
-    def product(ref):
+def pair_kernel(core_ref, *refs):
+    core, out_ref = core_ref[0], refs[-1]
+    own, other, right = refs[0:2], refs[2:4], refs[4:6]
+
+    def product(left):
         total = jnp.zeros((HALF, 2 * HALF), jnp.float32)
         for index in range(12):
-            total += lax.dot_general(
-                ref[index], right_ref[index], (((1,), (1,)), ((), ())), preferred_element_type=jnp.float32
+            rows = jnp.concatenate([ref[index] for ref in left], axis=0)
+            columns = jnp.concatenate(
+                [ref[index, pl.ds(part * PART, PART), :] for part in range(2) for ref in right], axis=0
             )
+            total += lax.dot_general(rows, columns, (((1,), (1,)), ((), ())), preferred_element_type=jnp.float32)
         return total.astype(jnp.bfloat16)
 
-    out_ref[pl.ds(pl.multiple_of(core * HALF, HALF), HALF), :] = product(own_ref)
-    out_ref[pl.ds(pl.multiple_of((1 - core) * HALF, HALF), HALF), :] = product(other_ref)
+    out_ref[pl.ds(pl.multiple_of(core * HALF, HALF), HALF), :] = product(own)
+    out_ref[pl.ds(pl.multiple_of((1 - core) * HALF, HALF), HALF), :] = product(other)
 
 
 def pair(core, own, other, right):
     return pl.pallas_call(
         pair_kernel,
         out_shape=jax.ShapeDtypeStruct((NV, 2 * HALF), jnp.bfloat16),
-        in_specs=[scalar(), whole(), whole(), whole()],
+        in_specs=[scalar()] + [whole()] * 6,
         out_specs=whole(),
         compiler_params=room(8),
         name="pair",
-    )(core, own, other, right)
+    )(core, *own, *other, *right)
 
 
 def spread_kernel(level_ref, source_ref, gathered_ref, out_ref):
@@ -340,9 +358,9 @@
         half = lax.dynamic_slice_in_dim(planes_here, index * HALF, HALF, 1).reshape(VROWS, SITES)
         return jnp.concatenate([half, tail], axis=0)
 
-    first_half, second_half = lax.optimization_barrier((half_of(core), half_of(1 - core)))
-    cross_sibling = lax.ppermute(second_half, sites, [(1, 2), (2, 1)])
-    cross_same = lax.ppermute(first_half, sites, [(1, 0), (2, 3)])
+    def part_of(index, turn):
+        rows = lax.dynamic_slice_in_dim(planes_here, index * HALF + turn * PART, PART, 1).reshape(PROWS, SITES)
+        return rows if turn else jnp.concatenate([rows, tail], axis=0)
 
     def moved(plane, distance):
         route = [
@@ -350,16 +368,28 @@
         ]
         return lax.ppermute(plane, SPACE, route)
 
+    sends = [(part_of(1 - core, turn), part_of(core, turn)) for turn in range(PARTS)]
+    first_half, second_half, sends = lax.optimization_barrier((half_of(core), half_of(1 - core), sends))
+    other = []
+    for turn in range(PARTS):
+        cross_sibling = lax.ppermute(sends[turn][0], sites, [(1, 2), (2, 1)])
+        cross_same = lax.ppermute(sends[turn][1], sites, [(1, 0), (2, 3)])
+        other.append((cross_sibling, cross_same))
     taken = lax.ppermute(second_half, sites, [(0, 2), (3, 1)])
     own = jnp.where(same, first_half, taken)
     row_own = (moved(own, 1), own, moved(own, -1), moved(own, -2))
-    other = jnp.where(same, cross_same, cross_sibling)
-    row_other = (moved(other, 1), other, moved(other, -1))
-    planes = [row_own[0], row_other[0], row_own[1], row_other[1], row_own[2], row_other[2], row_own[3]]
+    row_other = []
+    for turn in range(PARTS):
+        plane = jnp.where(same, other[turn][1], other[turn][0])
+        row_other.append((moved(plane, 1), plane, moved(plane, -1)))
     pick = row_own[1][VROWS + 54, 0].astype(jnp.int32)
     phase = phases(momentum, pick, pair_index, level, 2 * pairs)
-    left, right = smear(pick[None], level[None], phase, *planes)
-    sibling = lax.ppermute(left, "core", [(0, 1), (1, 0)])
+    left, right, sibling = [], [], []
+    for turn in range(PARTS):
+        results = smear(turn, pick[None], level[None], phase, row_own, row_other[turn], row_other[0])
+        left.append(results[0])
+        right.append(results[1])
+        sibling.append(lax.ppermute(results[0], "core", [(0, 1), (1, 0)]))
     partial_value = pair(core[None], left, sibling, right)
 
     parts = lax.all_to_all(partial_value, XY, 0, 0, tiled=True).reshape(pairs, rows, 2 * HALF)

time: 162 us -> 170 us (1.049)
  starting transfers between devices: 55.5 us -> 80.1 us
  waiting for transfers between devices: 68.2 us -> 52.4 us
    ppermute x3 -> x6, waiting for transfers between devices: 19.2 us -> 1.33 us  [the longest x2 1.32 us: per_device(): sibling.append(lax.ppermute(results[0], 'core', [(0, 1), (1, 0)]))]
    ppermute x1, starting transfers between devices: 16.2 us -> 27.9 us  [per_device(): taken = lax.ppermute(second_half, sites, [(0, 2), (3, 1)])]
    ppermute x5 -> x7, starting transfers between devices: 20.2 us -> 30.1 us  [moved(): return lax.ppermute(plane, SPACE, route)]
    ppermute x3 -> x6, starting transfers between devices: 3.89 us -> 8.25 us  [the longest x2 4.33 us: per_device(): sibling.append(lax.ppermute(results[0], 'core', [(0, 1), (1, 0)]))]
    ppermute x5 -> x7, waiting for transfers between devices: 5.91 us -> 8.12 us  [moved(): return lax.ppermute(plane, SPACE, route)]
    pallas_call x1 -> x2, Pallas kernels: 6.8 us -> 6.94 us  [smear(): pl.pallas_call(functools.partial(smear_kernel, turn), out_shape=(jax.Shap...]
  transfers between devices with their start and end apart: 12 -> 17, of which waited for: 7 -> 6; matrix products, arithmetic and copies ran while one was open for 3% -> 2% of each run, Pallas kernels for 0% -> 2%
where the time goes in v1:
time: 170 us; the launch traced here: 169 us
  starting transfers between devices  80.1 us (47%)
  waiting for transfers between devices  52.4 us (31%)
  Pallas kernels  13.2 us (8%)
  blocking collectives  10.8 us (6%)
  local copies, waits for them, and re-layouts  5.02 us (3%)
  between operations  4.15 us (2%)
  other arithmetic  3.75 us (2%)
    ppermute x7, starting transfers between devices, moved(): return lax.ppermute(plane, SPACE, route)  30.1 us
    ppermute x1, starting transfers between devices, per_device(): taken = lax.ppermute(second_half, sites, [(0, 2), (3, 1)])  27.9 us
    all_to_all x1, waiting for transfers between devices, per_device(): lax.all_to_all(value, SPACE, 0, 0, tiled=True)[:, :2].reshape(pairs, 2, 2)  16.2 us
    all_to_all x1, waiting for transfers between devices, per_device(): gathered = lax.all_to_all(copies, ('zl', 'zh'), 0, 0, tiled=True)  14.9 us
    all_to_all x1, waiting for transfers between devices, per_device(): arrived = lax.all_to_all(sent, ('core', 'y', 'x'), 0, 0, tiled=True)  11.9 us
    all_to_all x1, blocking collectives, per_device(): lax.all_to_all(partial_value, XY, 0, 0, tiled=True)  10.8 us
    ppermute x7, waiting for transfers between devices, moved(): return lax.ppermute(plane, SPACE, route)  8.12 us
    pallas_call x2, Pallas kernels, smear(): pl.pallas_call(functools.partial(smear_kernel, turn), out_shape=(jax.Shap...  6.94 us
  transfers between devices with their start and end apart: 17, of which 6 were waited for; matrix products, arithmetic and copies ran while one was open for 2% of the time, Pallas kernels for 2%

profile of v1, /device:TPU:32, one launch (start us, length us, event | category | flops | bytes accessed | tf_op | source)
XLA Modules:
  0.0 169.4 jit_solution(13026851317958574032)
XLA Ops:
  8.3 27.9 %collective-permute-start = (bf16[832,128]{1,0:T(8,128)(2,1)S(1)}, bf16[832,128]{1,0:T(8,128)(2,1)S(1)}, u32[]{:S(2)}, u32[]{:S(2)}) collective-permute-start(bf16[832,128]{1,0:T(8,128)(2,1)S(1)} %get-tuple-element.13), channel_id=1, source_target_pairs={{0,32},{33,1},{2,34},{35,3},{4,36},{37,5},{6,38},{39,7},{8,40},{41... | collective-permute-start | bytes 638984 | tf_op jit(solution)/shard_map/ppermute | solution.py:378
  40.7 7.1 %collective-permute-start.11 = (bf16[384,128]{1,0:T(8,128)(2,1)S(1)}, bf16[384,128]{1,0:T(8,128)(2,1)S(1)}, u32[]{:S(2)}, u32[]{:S(2)}) collective-permute-start(bf16[384,128]{1,0:T(8,128)(2,1)S(1)} %broadcast_select_fusion.2.refs_5_), channel_id=1, source_target_pairs={{0,30},{1,3},{2,0},{3,5},{4,2},{5,7},{6,4},{7,9},{8,6},{9,11},{10,... | collective-permute-start | bytes 294920 | tf_op jit(solution)/shard_map/ppermute | solution.py:369
  47.8 1.9 %collective-permute-start.10 = (bf16[384,128]{1,0:T(8,128)(2,1)S(1)}, bf16[384,128]{1,0:T(8,128)(2,1)S(1)}, u32[]{:S(2)}, u32[]{:S(2)}) collective-permute-start(bf16[384,128]{1,0:T(8,128)(2,1)S(1)} %broadcast_select_fusion.2.refs_5_), channel_id=1, source_target_pairs={{0,2},{1,31},{2,4},{3,1},{4,6},{5,3},{6,8},{7,5},{8,10},{9,7},{10,... | collective-permute-start | bytes 294920 | tf_op jit(solution)/shard_map/ppermute | solution.py:369
  49.8 7.2 %collective-permute-start.7 = (bf16[448,128]{1,0:T(8,128)(2,1)S(1)}, bf16[448,128]{1,0:T(8,128)(2,1)S(1)}, u32[]{:S(2)}, u32[]{:S(2)}) collective-permute-start(bf16[448,128]{1,0:T(8,128)(2,1)S(1)} %broadcast_select_fusion.1.refs_5_.refs_8_), channel_id=1, source_target_pairs={{0,30},{1,3},{2,0},{3,5},{4,2},{5,7},{6,4},{7,9},{8,6},{9,11},{10,... | collective-permute-start | bytes 344072 | tf_op jit(solution)/shard_map/ppermute | solution.py:369
  57.1 1.9 %collective-permute-start.6 = (bf16[448,128]{1,0:T(8,128)(2,1)S(1)}, bf16[448,128]{1,0:T(8,128)(2,1)S(1)}, u32[]{:S(2)}, u32[]{:S(2)}) collective-permute-start(bf16[448,128]{1,0:T(8,128)(2,1)S(1)} %broadcast_select_fusion.1.refs_5_.refs_8_), channel_id=1, source_target_pairs={{0,2},{1,31},{2,4},{3,1},{4,6},{5,3},{6,8},{7,5},{8,10},{9,7},{10,... | collective-permute-start | bytes 344072 | tf_op jit(solution)/shard_map/ppermute | solution.py:369
  59.6 3.4 %collective-permute-start.3 = (bf16[832,128]{1,0:T(8,128)(2,1)S(1)}, bf16[832,128]{1,0:T(8,128)(2,1)S(1)}, u32[]{:S(2)}, u32[]{:S(2)}) collective-permute-start(bf16[832,128]{1,0:T(8,128)(2,1)S(1)} %broadcast_select_fusion.refs_1_), channel_id=1, source_target_pairs={{0,28},{1,5},{2,30},{3,7},{4,0},{5,9},{6,2},{7,11},{8,4},{9,13},{1... | collective-permute-start | bytes 638984 | tf_op jit(solution)/shard_map/ppermute | solution.py:369
  63.5 5.8 %collective-permute-start.2 = (bf16[832,128]{1,0:T(8,128)(2,1)S(1)}, bf16[832,128]{1,0:T(8,128)(2,1)S(1)}, u32[]{:S(2)}, u32[]{:S(2)}) collective-permute-start(bf16[832,128]{1,0:T(8,128)(2,1)S(1)} %broadcast_select_fusion.refs_1_), channel_id=1, source_target_pairs={{0,30},{1,3},{2,0},{3,5},{4,2},{5,7},{6,4},{7,9},{8,6},{9,11},{10,... | collective-permute-start | bytes 638984 | tf_op jit(solution)/shard_map/ppermute | solution.py:369
  69.3 2.8 %collective-permute-start.1 = (bf16[832,128]{1,0:T(8,128)(2,1)S(1)}, bf16[832,128]{1,0:T(8,128)(2,1)S(1)}, u32[]{:S(2)}, u32[]{:S(2)}) collective-permute-start(bf16[832,128]{1,0:T(8,128)(2,1)S(1)} %broadcast_select_fusion.refs_1_), channel_id=1, source_target_pairs={{0,2},{1,31},{2,4},{3,1},{4,6},{5,3},{6,8},{7,5},{8,10},{9,7},{10,... | collective-permute-start | bytes 638984 | tf_op jit(solution)/shard_map/ppermute | solution.py:369
  72.3 3.5 %collective-permute-done.2.refs_2_ = bf16[832,128]{1,0:T(8,128)(2,1)S(1)} collective-permute-done((bf16[832,128]{1,0:T(8,128)(2,1)S(1)}, bf16[832,128]{1,0:T(8,128)(2,1)S(1)}, u32[]{:S(2)}, u32[]{:S(2)}) %collective-permute-start.2) | collective-permute-done | bytes 213024 | tf_op jit(solution)/shard_map/ppermute | solution.py:369
  75.8 4.6 %collective-permute-done.1.refs_0_ = bf16[832,128]{1,0:T(8,128)(2,1)S(1)} collective-permute-done((bf16[832,128]{1,0:T(8,128)(2,1)S(1)}, bf16[832,128]{1,0:T(8,128)(2,1)S(1)}, u32[]{:S(2)}, u32[]{:S(2)}) %collective-permute-start.1) | collective-permute-done | bytes 213024 | tf_op jit(solution)/shard_map/ppermute | solution.py:369
  80.4 3.5 %smear.3 = (bf16[12,64,256]{2,1,0:T(8,128)(2,1)S(1)}, bf16[12,128,256]{2,1,0:T(8,128)(2,1)S(1)}) custom-call(s32[1]{0:T(128)} %bitcast.10.pick_ref, s32[1]{0:T(128)} %bitcast.11.level_ref, f32[8,128]{1,0:T(8,128)S(1)} %bitcast.40, bf16[832,128]{1,0:T(8,128)(2,1)S(1)} %collective-permute-done.1.refs_0_, bf16[832,128]{1,0:T(8,128)(2,1)S(1)} %broadcast_select_fusion.refs_1_, ...), custom_call_target="tpu_custom_call" | custom-call | flops 10000000 | bytes 10000000 | tf_op jit(solution)/shard_map/smear/pallas_call | solution.py:206
  83.9 1.9 %collective-permute-start.13 = (bf16[12,64,256]{2,1,0:T(8,128)(2,1)S(1)}, bf16[12,64,256]{2,1,0:T(8,128)(2,1)S(1)}, u32[]{:S(2)}, u32[]{:S(2)}) collective-permute-start(bf16[12,64,256]{2,1,0:T(8,128)(2,1)S(1)} %get-tuple-element.19.refs_1_), channel_id=1, source_target_pairs={{0,32},{32,0},{1,33},{33,1},{2,34},{34,2},{3,35},{35,3},{4,36},{36... | collective-permute-start | bytes 1179656 | tf_op jit(solution)/shard_map/ppermute | solution.py:392
  85.8 3.5 %smear.2 = (bf16[12,64,256]{2,1,0:T(8,128)(2,1)S(1)}, bf16[12,128,256]{2,1,0:T(8,128)(2,1)S(1)}) custom-call(s32[1]{0:T(128)} %bitcast.10.pick_ref, s32[1]{0:T(128)} %bitcast.11.level_ref, f32[8,128]{1,0:T(8,128)S(1)} %bitcast.41, bf16[832,128]{1,0:T(8,128)(2,1)S(1)} %collective-permute-done.1.refs_0_, bf16[832,128]{1,0:T(8,128)(2,1)S(1)} %broadcast_select_fusion.refs_1_, ...), custom_call_target="tpu_custom_call" | custom-call | flops 10000000 | bytes 10000000 | tf_op jit(solution)/shard_map/smear/pallas_call | solution.py:206
  89.3 2.4 %collective-permute-start.12 = (bf16[12,64,256]{2,1,0:T(8,128)(2,1)S(1)}, bf16[12,64,256]{2,1,0:T(8,128)(2,1)S(1)}, u32[]{:S(2)}, u32[]{:S(2)}) collective-permute-start(bf16[12,64,256]{2,1,0:T(8,128)(2,1)S(1)} %get-tuple-element.16.refs_0_), channel_id=1, source_target_pairs={{0,32},{32,0},{1,33},{33,1},{2,34},{34,2},{3,35},{35,3},{4,36},{36... | collective-permute-start | bytes 1179656 | tf_op jit(solution)/shard_map/ppermute | solution.py:392
  91.7 1.3 collective-permute-done.12.refs_2_
  94.2 10.8 %all_to_all.31 = bf16[16,16,256]{2,1,0:T(8,128)(2,1)S(1)} all-to-all(bf16[16,16,256]{2,1,0:T(8,128)(2,1)S(1)} %bitcast.39), channel_id=1, replica_groups=mesh['zl'=8,'core'=2,'y'=4,'x'=4,'zh'=2] {'y','x'}, dimensions={0} | all-to-all | bytes 262144 | tf_op jit(solution)/shard_map/all_to_all | solution.py:395
  105.7 6.0 %all-to-all-start.1 = ((bf16[16,16,256]{2,1,0:T(8,128)(2,1)}), bf16[16,16,256]{2,1,0:T(8,128)(2,1)S(1)}, u32[]{:S(2)}, u32[]{:S(2)}) async-start(bf16[16,16,256]{2,1,0:T(8,128)(2,1)} %broadcast_in_dim.38), calls=%async_computation.1 | async-start | bytes 262144 | tf_op jit(solution)/shard_map/all_to_all | solution.py:401
  111.7 14.9 %all-to-all-done.1.gathered_ref = bf16[16,16,256]{2,1,0:T(8,128)(2,1)S(1)} async-done(((bf16[16,16,256]{2,1,0:T(8,128)(2,1)}), bf16[16,16,256]{2,1,0:T(8,128)(2,1)S(1)}, u32[]{:S(2)}, u32[]{:S(2)}) %all-to-all-start.1) | async-done | bytes 131104 | tf_op jit(solution)/shard_map/all_to_all | solution.py:401
  126.6 1.4 spread.1
  128.0 3.9 %all-to-all-start.2 = ((bf16[32,2,16,256]{3,2,1,0:T(8,128)(2,1)}), bf16[32,2,16,256]{3,2,1,0:T(8,128)(2,1)S(1)}, u32[]{:S(2)}, u32[]{:S(2)}) async-start(bf16[32,2,16,256]{3,2,1,0:T(8,128)(2,1)} %spread.1), calls=%async_computation.2 | async-start | bytes 1048576 | tf_op jit(solution)/shard_map/all_to_all | solution.py:403
  132.0 11.9 %all-to-all-done.2.arrived_ref = bf16[32,2,16,256]{3,2,1,0:T(8,128)(2,1)S(1)} async-done(((bf16[32,2,16,256]{3,2,1,0:T(8,128)(2,1)}), bf16[32,2,16,256]{3,2,1,0:T(8,128)(2,1)S(1)}, u32[]{:S(2)}, u32[]{:S(2)}) %all-to-all-start.2) | async-done | bytes 524320 | tf_op jit(solution)/shard_map/all_to_all | solution.py:403
  144.2 3.7 %trace.1 = f32[32,128]{1,0:T(8,128)} custom-call(bf16[32,2,16,256]{3,2,1,0:T(8,128)(2,1)S(1)} %all-to-all-done.2.arrived_ref, bf16[8,512,256]{2,1,0:T(8,128)(2,1)S(1)} %bitcast.38), custom_call_target="tpu_custom_call" | custom-call | tf_op jit(solution)/shard_map/trace/pallas_call | solution.py:314
  148.0 3.8 %all-to-all-start.3 = ((f32[32,1,128]{2,1,0:T(1,128)}), f32[32,1,128]{2,1,0:T(1,128)S(1)}, u32[]{:S(2)}, u32[]{:S(2)}) async-start(f32[32,1,128]{2,1,0:T(1,128)} %bitcast.25), calls=%async_computation.3 | async-start | bytes 32768 | tf_op jit(solution)/shard_map/all_to_all | solution.py:408
  152.5 16.2 %all-to-all-done.3 = f32[32,1,128]{2,1,0:T(1,128)S(1)} async-done(((f32[32,1,128]{2,1,0:T(1,128)}), f32[32,1,128]{2,1,0:T(1,128)S(1)}, u32[]{:S(2)}, u32[]{:S(2)}) %all-to-all-start.3) | async-done | bytes 16416 | tf_op jit(solution)/shard_map/all_to_all | solution.py:408
  (54 shorter events, 13.8 us)
Async XLA Ops:
  0.6 35.7 %copy-start.2 = (s32[3]{0:T(128)S(1)}, s32[3]{0:T(128)}, u32[]{:S(2)}) copy-start(s32[3]{0:T(128)} %param.10) | copy-start | bytes 40
  4.4 36.3 %collective-permute-start.8 = (bf16[384,128]{1,0:T(8,128)(2,1)S(1)}, bf16[384,128]{1,0:T(8,128)(2,1)S(1)}, u32[]{:S(2)}, u32[]{:S(2)}) collective-permute-start(bf16[384,128]{1,0:T(8,128)(2,1)S(1)} %bitcast.49), channel_id=1, source_target_pairs={{1,0},{32,33},{3,2},{34,35},{5,4},{36,37},{7,6},{38,39},{9,8},{40,... | collective-permute-start | bytes 294920 | tf_op jit(solution)/shard_map/ppermute | solution.py:376
  5.7 35.0 %collective-permute-start.9 = (bf16[384,128]{1,0:T(8,128)(2,1)S(1)}, bf16[384,128]{1,0:T(8,128)(2,1)S(1)}, u32[]{:S(2)}, u32[]{:S(2)}) collective-permute-start(bf16[384,128]{1,0:T(8,128)(2,1)S(1)} %bitcast.48), channel_id=1, source_target_pairs={{1,32},{32,1},{3,34},{34,3},{5,36},{36,5},{7,38},{38,7},{9,40},{40... | collective-permute-start | bytes 294920 | tf_op jit(solution)/shard_map/ppermute | solution.py:375
  6.4 43.4 %collective-permute-start.4 = (bf16[448,128]{1,0:T(8,128)(2,1)S(1)}, bf16[448,128]{1,0:T(8,128)(2,1)S(1)}, u32[]{:S(2)}, u32[]{:S(2)}) collective-permute-start(bf16[448,128]{1,0:T(8,128)(2,1)S(1)} %get-tuple-element.14), channel_id=1, source_target_pairs={{1,0},{32,33},{3,2},{34,35},{5,4},{36,37},{7,6},{38,39},{9,8},{40,... | collective-permute-start | bytes 344072 | tf_op jit(solution)/shard_map/ppermute | solution.py:376
  7.7 42.1 %collective-permute-start.5 = (bf16[448,128]{1,0:T(8,128)(2,1)S(1)}, bf16[448,128]{1,0:T(8,128)(2,1)S(1)}, u32[]{:S(2)}, u32[]{:S(2)}) collective-permute-start(bf16[448,128]{1,0:T(8,128)(2,1)S(1)} %get-tuple-element.15), channel_id=1, source_target_pairs={{1,32},{32,1},{3,34},{34,3},{5,36},{36,5},{7,38},{38,7},{9,40},{40... | collective-permute-start | bytes 344072 | tf_op jit(solution)/shard_map/ppermute | solution.py:375
  8.3 50.6 %collective-permute-start = (bf16[832,128]{1,0:T(8,128)(2,1)S(1)}, bf16[832,128]{1,0:T(8,128)(2,1)S(1)}, u32[]{:S(2)}, u32[]{:S(2)}) collective-permute-start(bf16[832,128]{1,0:T(8,128)(2,1)S(1)} %get-tuple-element.13), channel_id=1, source_target_pairs={{0,32},{33,1},{2,34},{35,3},{4,36},{37,5},{6,38},{39,7},{8,40},{41... | collective-permute-start | bytes 638984 | tf_op jit(solution)/shard_map/ppermute | solution.py:378
  40.7 22.8 %collective-permute-start.11 = (bf16[384,128]{1,0:T(8,128)(2,1)S(1)}, bf16[384,128]{1,0:T(8,128)(2,1)S(1)}, u32[]{:S(2)}, u32[]{:S(2)}) collective-permute-start(bf16[384,128]{1,0:T(8,128)(2,1)S(1)} %broadcast_select_fusion.2.refs_5_), channel_id=1, source_target_pairs={{0,30},{1,3},{2,0},{3,5},{4,2},{5,7},{6,4},{7,9},{8,6},{9,11},{10,... | collective-permute-start | bytes 294920 | tf_op jit(solution)/shard_map/ppermute | solution.py:369
  47.8 21.5 %collective-permute-start.10 = (bf16[384,128]{1,0:T(8,128)(2,1)S(1)}, bf16[384,128]{1,0:T(8,128)(2,1)S(1)}, u32[]{:S(2)}, u32[]{:S(2)}) collective-permute-start(bf16[384,128]{1,0:T(8,128)(2,1)S(1)} %broadcast_select_fusion.2.refs_5_), channel_id=1, source_target_pairs={{0,2},{1,31},{2,4},{3,1},{4,6},{5,3},{6,8},{7,5},{8,10},{9,7},{10,... | collective-permute-start | bytes 294920 | tf_op jit(solution)/shard_map/ppermute | solution.py:369
  49.8 22.4 %collective-permute-start.7 = (bf16[448,128]{1,0:T(8,128)(2,1)S(1)}, bf16[448,128]{1,0:T(8,128)(2,1)S(1)}, u32[]{:S(2)}, u32[]{:S(2)}) collective-permute-start(bf16[448,128]{1,0:T(8,128)(2,1)S(1)} %broadcast_select_fusion.1.refs_5_.refs_8_), channel_id=1, source_target_pairs={{0,30},{1,3},{2,0},{3,5},{4,2},{5,7},{6,4},{7,9},{8,6},{9,11},{10,... | collective-permute-start | bytes 344072 | tf_op jit(solution)/shard_map/ppermute | solution.py:369
  57.1 15.2 %collective-permute-start.6 = (bf16[448,128]{1,0:T(8,128)(2,1)S(1)}, bf16[448,128]{1,0:T(8,128)(2,1)S(1)}, u32[]{:S(2)}, u32[]{:S(2)}) collective-permute-start(bf16[448,128]{1,0:T(8,128)(2,1)S(1)} %broadcast_select_fusion.1.refs_5_.refs_8_), channel_id=1, source_target_pairs={{0,2},{1,31},{2,4},{3,1},{4,6},{5,3},{6,8},{7,5},{8,10},{9,7},{10,... | collective-permute-start | bytes 344072 | tf_op jit(solution)/shard_map/ppermute | solution.py:369
  59.6 12.7 %collective-permute-start.3 = (bf16[832,128]{1,0:T(8,128)(2,1)S(1)}, bf16[832,128]{1,0:T(8,128)(2,1)S(1)}, u32[]{:S(2)}, u32[]{:S(2)}) collective-permute-start(bf16[832,128]{1,0:T(8,128)(2,1)S(1)} %broadcast_select_fusion.refs_1_), channel_id=1, source_target_pairs={{0,28},{1,5},{2,30},{3,7},{4,0},{5,9},{6,2},{7,11},{8,4},{9,13},{1... | collective-permute-start | bytes 638984 | tf_op jit(solution)/shard_map/ppermute | solution.py:369
  63.5 12.3 %collective-permute-start.2 = (bf16[832,128]{1,0:T(8,128)(2,1)S(1)}, bf16[832,128]{1,0:T(8,128)(2,1)S(1)}, u32[]{:S(2)}, u32[]{:S(2)}) collective-permute-start(bf16[832,128]{1,0:T(8,128)(2,1)S(1)} %broadcast_select_fusion.refs_1_), channel_id=1, source_target_pairs={{0,30},{1,3},{2,0},{3,5},{4,2},{5,7},{6,4},{7,9},{8,6},{9,11},{10,... | collective-permute-start | bytes 638984 | tf_op jit(solution)/shard_map/ppermute | solution.py:369
  69.3 11.1 %collective-permute-start.1 = (bf16[832,128]{1,0:T(8,128)(2,1)S(1)}, bf16[832,128]{1,0:T(8,128)(2,1)S(1)}, u32[]{:S(2)}, u32[]{:S(2)}) collective-permute-start(bf16[832,128]{1,0:T(8,128)(2,1)S(1)} %broadcast_select_fusion.refs_1_), channel_id=1, source_target_pairs={{0,2},{1,31},{2,4},{3,1},{4,6},{5,3},{6,8},{7,5},{8,10},{9,7},{10,... | collective-permute-start | bytes 638984 | tf_op jit(solution)/shard_map/ppermute | solution.py:369
  83.9 7.8 %collective-permute-start.13 = (bf16[12,64,256]{2,1,0:T(8,128)(2,1)S(1)}, bf16[12,64,256]{2,1,0:T(8,128)(2,1)S(1)}, u32[]{:S(2)}, u32[]{:S(2)}) collective-permute-start(bf16[12,64,256]{2,1,0:T(8,128)(2,1)S(1)} %get-tuple-element.19.refs_1_), channel_id=1, source_target_pairs={{0,32},{32,0},{1,33},{33,1},{2,34},{34,2},{3,35},{35,3},{4,36},{36... | collective-permute-start | bytes 1179656 | tf_op jit(solution)/shard_map/ppermute | solution.py:392
  89.3 37.4 %copy-start.1 = (s32[16]{0:T(128)S(1)}, s32[16]{0:T(128)}, u32[]{:S(2)}) copy-start(s32[16]{0:T(128)} %source_ref.1) | copy-start | bytes 196
  89.3 3.7 %collective-permute-start.12 = (bf16[12,64,256]{2,1,0:T(8,128)(2,1)S(1)}, bf16[12,64,256]{2,1,0:T(8,128)(2,1)S(1)}, u32[]{:S(2)}, u32[]{:S(2)}) collective-permute-start(bf16[12,64,256]{2,1,0:T(8,128)(2,1)S(1)} %get-tuple-element.16.refs_0_), channel_id=1, source_target_pairs={{0,32},{32,0},{1,33},{33,1},{2,34},{34,2},{3,35},{35,3},{4,36},{36... | collective-permute-start | bytes 1179656 | tf_op jit(solution)/shard_map/ppermute | solution.py:392
  94.2 50.1 %copy-start = (bf16[1,8,2,256,256]{4,3,2,1,0:T(8,128)(2,1)S(1)}, bf16[1,8,2,256,256]{4,3,2,1,0:T(8,128)(2,1)}, u32[]{:S(2)}) copy-start(bf16[1,8,2,256,256]{4,3,2,1,0:T(8,128)(2,1)} %param.8) | copy-start | bytes 6291460
  105.7 21.0 %all-to-all-start.1 = ((bf16[16,16,256]{2,1,0:T(8,128)(2,1)}), bf16[16,16,256]{2,1,0:T(8,128)(2,1)S(1)}, u32[]{:S(2)}, u32[]{:S(2)}) async-start(bf16[16,16,256]{2,1,0:T(8,128)(2,1)} %broadcast_in_dim.38), calls=%async_computation.1 | async-start | bytes 262144 | tf_op jit(solution)/shard_map/all_to_all | solution.py:401
  128.0 15.9 %all-to-all-start.2 = ((bf16[32,2,16,256]{3,2,1,0:T(8,128)(2,1)}), bf16[32,2,16,256]{3,2,1,0:T(8,128)(2,1)S(1)}, u32[]{:S(2)}, u32[]{:S(2)}) async-start(bf16[32,2,16,256]{3,2,1,0:T(8,128)(2,1)} %spread.1), calls=%async_computation.2 | async-start | bytes 1048576 | tf_op jit(solution)/shard_map/all_to_all | solution.py:403
  148.0 20.7 %all-to-all-start.3 = ((f32[32,1,128]{2,1,0:T(1,128)}), f32[32,1,128]{2,1,0:T(1,128)S(1)}, u32[]{:S(2)}, u32[]{:S(2)}) async-start(f32[32,1,128]{2,1,0:T(1,128)} %bitcast.25), calls=%async_computation.3 | async-start | bytes 32768 | tf_op jit(solution)/shard_map/all_to_all | solution.py:408

commit v2 on v0

--- a/solution.py
+++ b/solution.py
@@ -20,7 +20,7 @@
 
 SPACE = ("y", "x", "zh")
 XY = ("y", "x")
-CHUNK = 16
+CHUNK = 32
 
 
 def whole():
@@ -357,7 +357,8 @@
     row_other = (moved(other, 1), other, moved(other, -1))
     planes = [row_own[0], row_other[0], row_own[1], row_other[1], row_own[2], row_other[2], row_own[3]]
     pick = row_own[1][VROWS + 54, 0].astype(jnp.int32)
-    phase = phases(momentum, pick, pair_index, level, 2 * pairs)
+    late_momentum, _ = lax.optimization_barrier((momentum, other))
+    phase = phases(late_momentum, pick, pair_index, level, 2 * pairs)
     left, right = smear(pick[None], level[None], phase, *planes)
     sibling = lax.ppermute(left, "core", [(0, 1), (1, 0)])
     partial_value = pair(core[None], left, sibling, right)

time: 162 us -> 163 us (level)
  starting transfers between devices: 55.5 us -> 76.7 us
  waiting for transfers between devices: 68.2 us -> 48.5 us
    ppermute x1, starting transfers between devices: 1.92 us -> 16.6 us  [per_device(): sibling = lax.ppermute(left, 'core', [(0, 1), (1, 0)])]
    ppermute x1, waiting for transfers between devices: 16.9 us -> 2.38 us  [per_device(): cross_same = lax.ppermute(first_half, sites, [(1, 0), (2, 3)])]
    all_to_all x1, starting transfers between devices: 7.53 us -> 14 us  [per_device(): gathered = lax.all_to_all(copies, ('zl', 'zh'), 0, 0, tiled=True)]
    ppermute x5, waiting for transfers between devices: 5.91 us -> 2.08 us  [moved(): return lax.ppermute(plane, SPACE, route)]
  transfers between devices with their start and end apart: 12 -> 12, of which waited for: 7 -> 6; matrix products, arithmetic and copies ran while one was open for 3% -> 2% of each run, Pallas kernels for 0% -> 0%
where the time goes in v2:
time: 163 us; the launch traced here: 162 us
  starting transfers between devices  76.7 us (47%)
  waiting for transfers between devices  48.5 us (30%)
  Pallas kernels  12.9 us (8%)
  blocking collectives  11.8 us (7%)
  between operations  4.11 us (3%)
  local copies, waits for them, and re-layouts  4.04 us (2%)
  other arithmetic  3.87 us (2%)
    ppermute x5, starting transfers between devices, moved(): return lax.ppermute(plane, SPACE, route)  20.2 us
    ppermute x1, starting transfers between devices, per_device(): sibling = lax.ppermute(left, 'core', [(0, 1), (1, 0)])  16.6 us
    ppermute x1, starting transfers between devices, per_device(): taken = lax.ppermute(second_half, sites, [(0, 2), (3, 1)])  16.3 us
    all_to_all x1, waiting for transfers between devices, per_device(): lax.all_to_all(value, SPACE, 0, 0, tiled=True)[:, :2].reshape(pairs, 2, 2)  16.2 us
    all_to_all x1, waiting for transfers between devices, per_device(): gathered = lax.all_to_all(copies, ('zl', 'zh'), 0, 0, tiled=True)  14.1 us
    all_to_all x1, starting transfers between devices, per_device(): gathered = lax.all_to_all(copies, ('zl', 'zh'), 0, 0, tiled=True)  14 us
    all_to_all x1, waiting for transfers between devices, per_device(): arrived = lax.all_to_all(sent, ('core', 'y', 'x'), 0, 0, tiled=True)  11.9 us
    all_to_all x1, blocking collectives, per_device(): lax.all_to_all(partial_value, XY, 0, 0, tiled=True)  11.8 us
  transfers between devices with their start and end apart: 12, of which 6 were waited for; matrix products, arithmetic and copies ran while one was open for 2% of the time, Pallas kernels for 0%

profile of v2, /device:TPU:32, one launch (start us, length us, event | category | flops | bytes accessed | tf_op | source)
XLA Modules:
  0.0 161.9 jit_solution(2267774332198846459)
XLA Ops:
  2.2 1.0 constant_dynamic-slice_fusion.1
  3.5 1.3 collective-permute-start.1
  5.5 16.3 %collective-permute-start = (bf16[832,128]{1,0:T(8,128)(2,1)S(1)}, bf16[832,128]{1,0:T(8,128)(2,1)S(1)}, u32[]{:S(2)}, u32[]{:S(2)}) collective-permute-start(bf16[832,128]{1,0:T(8,128)(2,1)S(1)} %get-tuple-element.8), channel_id=1, source_target_pairs={{0,32},{33,1},{2,34},{35,3},{4,36},{37,5},{6,38},{39,7},{8,40},{41... | collective-permute-start | bytes 638984 | tf_op jit(solution)/shard_map/ppermute | solution.py:353
  21.7 2.4 %collective-permute-done.1 = bf16[832,128]{1,0:T(8,128)(2,1)S(1)} collective-permute-done((bf16[832,128]{1,0:T(8,128)(2,1)S(1)}, bf16[832,128]{1,0:T(8,128)(2,1)S(1)}, u32[]{:S(2)}, u32[]{:S(2)}) %collective-permute-start.1) | collective-permute-done | bytes 213024 | tf_op jit(solution)/shard_map/ppermute | solution.py:345
  24.2 3.4 %collective-permute-start.4 = (bf16[832,128]{1,0:T(8,128)(2,1)S(1)}, bf16[832,128]{1,0:T(8,128)(2,1)S(1)}, u32[]{:S(2)}, u32[]{:S(2)}) collective-permute-start(bf16[832,128]{1,0:T(8,128)(2,1)S(1)} %broadcast_select_fusion.refs_3_), channel_id=1, source_target_pairs={{0,2},{1,31},{2,4},{3,1},{4,6},{5,3},{6,8},{7,5},{8,10},{9,7},{10,... | collective-permute-start | bytes 638984 | tf_op jit(solution)/shard_map/ppermute | solution.py:351
  27.6 5.8 %collective-permute-start.6 = (bf16[832,128]{1,0:T(8,128)(2,1)S(1)}, bf16[832,128]{1,0:T(8,128)(2,1)S(1)}, u32[]{:S(2)}, u32[]{:S(2)}) collective-permute-start(bf16[832,128]{1,0:T(8,128)(2,1)S(1)} %broadcast_select_fusion.refs_3_), channel_id=1, source_target_pairs={{0,30},{1,3},{2,0},{3,5},{4,2},{5,7},{6,4},{7,9},{8,6},{9,11},{10,... | collective-permute-start | bytes 638984 | tf_op jit(solution)/shard_map/ppermute | solution.py:351
  33.9 1.9 %collective-permute-start.3 = (bf16[832,128]{1,0:T(8,128)(2,1)S(1)}, bf16[832,128]{1,0:T(8,128)(2,1)S(1)}, u32[]{:S(2)}, u32[]{:S(2)}) collective-permute-start(bf16[832,128]{1,0:T(8,128)(2,1)S(1)} %broadcast_select_fusion.1.refs_2_), channel_id=1, source_target_pairs={{0,2},{1,31},{2,4},{3,1},{4,6},{5,3},{6,8},{7,5},{8,10},{9,7},{10,... | collective-permute-start | bytes 638984 | tf_op jit(solution)/shard_map/ppermute | solution.py:351
  35.8 7.2 %collective-permute-start.5 = (bf16[832,128]{1,0:T(8,128)(2,1)S(1)}, bf16[832,128]{1,0:T(8,128)(2,1)S(1)}, u32[]{:S(2)}, u32[]{:S(2)}) collective-permute-start(bf16[832,128]{1,0:T(8,128)(2,1)S(1)} %broadcast_select_fusion.1.refs_2_), channel_id=1, source_target_pairs={{0,30},{1,3},{2,0},{3,5},{4,2},{5,7},{6,4},{7,9},{8,6},{9,11},{10,... | collective-permute-start | bytes 638984 | tf_op jit(solution)/shard_map/ppermute | solution.py:351
  43.1 1.9 %collective-permute-start.7 = (bf16[832,128]{1,0:T(8,128)(2,1)S(1)}, bf16[832,128]{1,0:T(8,128)(2,1)S(1)}, u32[]{:S(2)}, u32[]{:S(2)}) collective-permute-start(bf16[832,128]{1,0:T(8,128)(2,1)S(1)} %broadcast_select_fusion.1.refs_2_), channel_id=1, source_target_pairs={{0,28},{1,5},{2,30},{3,7},{4,0},{5,9},{6,2},{7,11},{8,4},{9,13},{1... | collective-permute-start | bytes 638984 | tf_op jit(solution)/shard_map/ppermute | solution.py:351
  46.9 1.3 fusion.9
  50.3 2.1 %collective-permute-done.7.refs_6_ = bf16[832,128]{1,0:T(8,128)(2,1)S(1)} collective-permute-done((bf16[832,128]{1,0:T(8,128)(2,1)S(1)}, bf16[832,128]{1,0:T(8,128)(2,1)S(1)}, u32[]{:S(2)}, u32[]{:S(2)}) %collective-permute-start.7) | collective-permute-done | bytes 213024 | tf_op jit(solution)/shard_map/ppermute | solution.py:351
  52.3 6.7 %smear.1 = (bf16[12,128,256]{2,1,0:T(8,128)(2,1)S(1)}, bf16[12,256,256]{2,1,0:T(8,128)(2,1)S(1)}) custom-call(s32[1]{0:T(128)} %bitcast.6.pick_ref, s32[1]{0:T(128)} %bitcast.7.level_ref, f32[8,128]{1,0:T(8,128)S(1)} %bitcast.36, bf16[832,128]{1,0:T(8,128)(2,1)S(1)} %collective-permute-done.3.refs_0_, bf16[832,128]{1,0:T(8,128)(2,1)S(1)} %collective-permute-done.4.refs_1_, ...), custom_call_target="tpu_custom_call" | custom-call | tf_op jit(solution)/shard_map/smear/pallas_call | solution.py:192
  59.1 16.6 %collective-permute-start.8 = (bf16[12,128,256]{2,1,0:T(8,128)(2,1)S(1)}, bf16[12,128,256]{2,1,0:T(8,128)(2,1)S(1)}, u32[]{:S(2)}, u32[]{:S(2)}) collective-permute-start(bf16[12,128,256]{2,1,0:T(8,128)(2,1)S(1)} %get-tuple-element.10.own_ref), channel_id=1, source_target_pairs={{0,32},{32,0},{1,33},{33,1},{2,34},{34,2},{3,35},{35,3},{4,36},{36... | collective-permute-start | bytes 2359304 | tf_op jit(solution)/shard_map/ppermute | solution.py:363
  75.6 1.9 %collective-permute-done.8.other_ref = bf16[12,128,256]{2,1,0:T(8,128)(2,1)S(1)} collective-permute-done((bf16[12,128,256]{2,1,0:T(8,128)(2,1)S(1)}, bf16[12,128,256]{2,1,0:T(8,128)(2,1)S(1)}, u32[]{:S(2)}, u32[]{:S(2)}) %collective-permute-start.8) | collective-permute-done | bytes 786464 | tf_op jit(solution)/shard_map/ppermute | solution.py:363
  77.5 1.1 pair.1
  78.7 11.8 %all_to_all.31 = bf16[16,16,256]{2,1,0:T(8,128)(2,1)S(1)} all-to-all(bf16[16,16,256]{2,1,0:T(8,128)(2,1)S(1)} %bitcast.35), channel_id=1, replica_groups=mesh['zl'=8,'core'=2,'y'=4,'x'=4,'zh'=2] {'y','x'}, dimensions={0} | all-to-all | bytes 262144 | tf_op jit(solution)/shard_map/all_to_all | solution.py:366
  91.1 14.0 %all-to-all-start.1 = ((bf16[16,16,256]{2,1,0:T(8,128)(2,1)}), bf16[16,16,256]{2,1,0:T(8,128)(2,1)S(1)}, u32[]{:S(2)}, u32[]{:S(2)}) async-start(bf16[16,16,256]{2,1,0:T(8,128)(2,1)} %broadcast_in_dim.36), calls=%async_computation.1 | async-start | bytes 262144 | tf_op jit(solution)/shard_map/all_to_all | solution.py:372
  105.1 14.1 %all-to-all-done.1.gathered_ref = bf16[16,16,256]{2,1,0:T(8,128)(2,1)S(1)} async-done(((bf16[16,16,256]{2,1,0:T(8,128)(2,1)}), bf16[16,16,256]{2,1,0:T(8,128)(2,1)S(1)}, u32[]{:S(2)}, u32[]{:S(2)}) %all-to-all-start.1) | async-done | bytes 131104 | tf_op jit(solution)/shard_map/all_to_all | solution.py:372
  119.2 1.4 spread.1
  120.5 3.9 %all-to-all-start.2 = ((bf16[32,2,16,256]{3,2,1,0:T(8,128)(2,1)}), bf16[32,2,16,256]{3,2,1,0:T(8,128)(2,1)S(1)}, u32[]{:S(2)}, u32[]{:S(2)}) async-start(bf16[32,2,16,256]{3,2,1,0:T(8,128)(2,1)} %spread.1), calls=%async_computation.2 | async-start | bytes 1048576 | tf_op jit(solution)/shard_map/all_to_all | solution.py:374
  124.5 11.9 %all-to-all-done.2.arrived_ref = bf16[32,2,16,256]{3,2,1,0:T(8,128)(2,1)S(1)} async-done(((bf16[32,2,16,256]{3,2,1,0:T(8,128)(2,1)}), bf16[32,2,16,256]{3,2,1,0:T(8,128)(2,1)S(1)}, u32[]{:S(2)}, u32[]{:S(2)}) %all-to-all-start.2) | async-done | bytes 524320 | tf_op jit(solution)/shard_map/all_to_all | solution.py:374
  136.7 3.7 %trace.1 = f32[32,128]{1,0:T(8,128)} custom-call(bf16[32,2,16,256]{3,2,1,0:T(8,128)(2,1)S(1)} %all-to-all-done.2.arrived_ref, bf16[8,512,256]{2,1,0:T(8,128)(2,1)S(1)} %bitcast.34), custom_call_target="tpu_custom_call" | custom-call | tf_op jit(solution)/shard_map/trace/pallas_call | solution.py:296
  140.5 3.8 %all-to-all-start.3 = ((f32[32,1,128]{2,1,0:T(1,128)}), f32[32,1,128]{2,1,0:T(1,128)S(1)}, u32[]{:S(2)}, u32[]{:S(2)}) async-start(f32[32,1,128]{2,1,0:T(1,128)} %bitcast.21), calls=%async_computation.3 | async-start | bytes 32768 | tf_op jit(solution)/shard_map/all_to_all | solution.py:379
  145.0 16.2 %all-to-all-done.3 = f32[32,1,128]{2,1,0:T(1,128)S(1)} async-done(((f32[32,1,128]{2,1,0:T(1,128)}), f32[32,1,128]{2,1,0:T(1,128)S(1)}, u32[]{:S(2)}, u32[]{:S(2)}) %all-to-all-start.3) | async-done | bytes 16416 | tf_op jit(solution)/shard_map/all_to_all | solution.py:379
  (41 shorter events, 6.3 us)
Async XLA Ops:
  0.6 44.4 %copy-start.2 = (s32[3]{0:T(128)S(1)}, s32[3]{0:T(128)}, u32[]{:S(2)}) copy-start(s32[3]{0:T(128)} %param.10) | copy-start | bytes 40
  3.5 20.6 %collective-permute-start.1 = (bf16[832,128]{1,0:T(8,128)(2,1)S(1)}, bf16[832,128]{1,0:T(8,128)(2,1)S(1)}, u32[]{:S(2)}, u32[]{:S(2)}) collective-permute-start(bf16[832,128]{1,0:T(8,128)(2,1)S(1)} %get-tuple-element.7), channel_id=1, source_target_pairs={{1,0},{32,33},{3,2},{34,35},{5,4},{36,37},{7,6},{38,39},{9,8},{40,... | collective-permute-start | bytes 638984 | tf_op jit(solution)/shard_map/ppermute | solution.py:345
  4.8 19.3 %collective-permute-start.2 = (bf16[832,128]{1,0:T(8,128)(2,1)S(1)}, bf16[832,128]{1,0:T(8,128)(2,1)S(1)}, u32[]{:S(2)}, u32[]{:S(2)}) collective-permute-start(bf16[832,128]{1,0:T(8,128)(2,1)S(1)} %get-tuple-element.8), channel_id=1, source_target_pairs={{1,32},{32,1},{3,34},{34,3},{5,36},{36,5},{7,38},{38,7},{9,40},{40... | collective-permute-start | bytes 638984 | tf_op jit(solution)/shard_map/ppermute | solution.py:344
  5.5 27.9 %collective-permute-start = (bf16[832,128]{1,0:T(8,128)(2,1)S(1)}, bf16[832,128]{1,0:T(8,128)(2,1)S(1)}, u32[]{:S(2)}, u32[]{:S(2)}) collective-permute-start(bf16[832,128]{1,0:T(8,128)(2,1)S(1)} %get-tuple-element.8), channel_id=1, source_target_pairs={{0,32},{33,1},{2,34},{35,3},{4,36},{37,5},{6,38},{39,7},{8,40},{41... | collective-permute-start | bytes 638984 | tf_op jit(solution)/shard_map/ppermute | solution.py:353
  24.2 26.1 %collective-permute-start.4 = (bf16[832,128]{1,0:T(8,128)(2,1)S(1)}, bf16[832,128]{1,0:T(8,128)(2,1)S(1)}, u32[]{:S(2)}, u32[]{:S(2)}) collective-permute-start(bf16[832,128]{1,0:T(8,128)(2,1)S(1)} %broadcast_select_fusion.refs_3_), channel_id=1, source_target_pairs={{0,2},{1,31},{2,4},{3,1},{4,6},{5,3},{6,8},{7,5},{8,10},{9,7},{10,... | collective-permute-start | bytes 638984 | tf_op jit(solution)/shard_map/ppermute | solution.py:351
  27.6 22.7 %collective-permute-start.6 = (bf16[832,128]{1,0:T(8,128)(2,1)S(1)}, bf16[832,128]{1,0:T(8,128)(2,1)S(1)}, u32[]{:S(2)}, u32[]{:S(2)}) collective-permute-start(bf16[832,128]{1,0:T(8,128)(2,1)S(1)} %broadcast_select_fusion.refs_3_), channel_id=1, source_target_pairs={{0,30},{1,3},{2,0},{3,5},{4,2},{5,7},{6,4},{7,9},{8,6},{9,11},{10,... | collective-permute-start | bytes 638984 | tf_op jit(solution)/shard_map/ppermute | solution.py:351
  33.9 16.3 %collective-permute-start.3 = (bf16[832,128]{1,0:T(8,128)(2,1)S(1)}, bf16[832,128]{1,0:T(8,128)(2,1)S(1)}, u32[]{:S(2)}, u32[]{:S(2)}) collective-permute-start(bf16[832,128]{1,0:T(8,128)(2,1)S(1)} %broadcast_select_fusion.1.refs_2_), channel_id=1, source_target_pairs={{0,2},{1,31},{2,4},{3,1},{4,6},{5,3},{6,8},{7,5},{8,10},{9,7},{10,... | collective-permute-start | bytes 638984 | tf_op jit(solution)/shard_map/ppermute | solution.py:351
  35.8 14.4 %collective-permute-start.5 = (bf16[832,128]{1,0:T(8,128)(2,1)S(1)}, bf16[832,128]{1,0:T(8,128)(2,1)S(1)}, u32[]{:S(2)}, u32[]{:S(2)}) collective-permute-start(bf16[832,128]{1,0:T(8,128)(2,1)S(1)} %broadcast_select_fusion.1.refs_2_), channel_id=1, source_target_pairs={{0,30},{1,3},{2,0},{3,5},{4,2},{5,7},{6,4},{7,9},{8,6},{9,11},{10,... | collective-permute-start | bytes 638984 | tf_op jit(solution)/shard_map/ppermute | solution.py:351
  43.1 9.2 %collective-permute-start.7 = (bf16[832,128]{1,0:T(8,128)(2,1)S(1)}, bf16[832,128]{1,0:T(8,128)(2,1)S(1)}, u32[]{:S(2)}, u32[]{:S(2)}) collective-permute-start(bf16[832,128]{1,0:T(8,128)(2,1)S(1)} %broadcast_select_fusion.1.refs_2_), channel_id=1, source_target_pairs={{0,28},{1,5},{2,30},{3,7},{4,0},{5,9},{6,2},{7,11},{8,4},{9,13},{1... | collective-permute-start | bytes 638984 | tf_op jit(solution)/shard_map/ppermute | solution.py:351
  59.0 60.1 %copy-start.1 = (s32[16]{0:T(128)S(1)}, s32[16]{0:T(128)}, u32[]{:S(2)}) copy-start(s32[16]{0:T(128)} %source_ref.1) | copy-start | bytes 196
  59.1 18.5 %collective-permute-start.8 = (bf16[12,128,256]{2,1,0:T(8,128)(2,1)S(1)}, bf16[12,128,256]{2,1,0:T(8,128)(2,1)S(1)}, u32[]{:S(2)}, u32[]{:S(2)}) collective-permute-start(bf16[12,128,256]{2,1,0:T(8,128)(2,1)S(1)} %get-tuple-element.10.own_ref), channel_id=1, source_target_pairs={{0,32},{32,0},{1,33},{33,1},{2,34},{34,2},{3,35},{35,3},{4,36},{36... | collective-permute-start | bytes 2359304 | tf_op jit(solution)/shard_map/ppermute | solution.py:363
  78.7 58.1 %copy-start = (bf16[1,8,2,256,256]{4,3,2,1,0:T(8,128)(2,1)S(1)}, bf16[1,8,2,256,256]{4,3,2,1,0:T(8,128)(2,1)}, u32[]{:S(2)}) copy-start(bf16[1,8,2,256,256]{4,3,2,1,0:T(8,128)(2,1)} %param.8) | copy-start | bytes 6291460
  91.1 28.0 %all-to-all-start.1 = ((bf16[16,16,256]{2,1,0:T(8,128)(2,1)}), bf16[16,16,256]{2,1,0:T(8,128)(2,1)S(1)}, u32[]{:S(2)}, u32[]{:S(2)}) async-start(bf16[16,16,256]{2,1,0:T(8,128)(2,1)} %broadcast_in_dim.36), calls=%async_computation.1 | async-start | bytes 262144 | tf_op jit(solution)/shard_map/all_to_all | solution.py:372
  120.5 15.9 %all-to-all-start.2 = ((bf16[32,2,16,256]{3,2,1,0:T(8,128)(2,1)}), bf16[32,2,16,256]{3,2,1,0:T(8,128)(2,1)S(1)}, u32[]{:S(2)}, u32[]{:S(2)}) async-start(bf16[32,2,16,256]{3,2,1,0:T(8,128)(2,1)} %spread.1), calls=%async_computation.2 | async-start | bytes 1048576 | tf_op jit(solution)/shard_map/all_to_all | solution.py:374
  140.5 20.7 %all-to-all-start.3 = ((f32[32,1,128]{2,1,0:T(1,128)}), f32[32,1,128]{2,1,0:T(1,128)S(1)}, u32[]{:S(2)}, u32[]{:S(2)}) async-start(f32[32,1,128]{2,1,0:T(1,128)} %bitcast.21), calls=%async_computation.3 | async-start | bytes 32768 | tf_op jit(solution)/shard_map/all_to_all | solution.py:379
